TPU v7x, 512 devices: a whole 4x8x8 slice. The times are simulated.
512 devices in a mesh: dp: 8 (over z), expert: 64 (over y, x, core).
Axes of the slice: x: 4, y: 8, z: 8, core: 2. Of those that a mesh axis runs over, the one named last changes fastest.
Arguments:
- tokens: bfloat16 [65536, 3584], P(('dp', 'expert')), may hold values from -6 to 6
- cotangent: bfloat16 [65536, 3584], P(('dp', 'expert')), may hold values from -6 to 6
- route_ids: int32 [65536, 8], P(('dp', 'expert')), may hold values from 0 to 255, as said below
- route_gates: float32 [65536, 8], P(('dp', 'expert')), may hold values from 0.1 to 1
- gate_w: bfloat16 [3584, 8192], P('dp', 'expert'), may hold values from -0.09375 to 0.09375
- up_w: bfloat16 [3584, 8192], P('dp', 'expert'), may hold values from -0.09375 to 0.09375
- down_w: bfloat16 [3584, 8192], P('dp', 'expert'), may hold values from -0.1875 to 0.1875
Outputs:
- moe_out: bfloat16 [65536, 3584], P(('dp', 'expert'))
- d_tokens: bfloat16 [65536, 3584], P(('dp', 'expert'))
- d_gates: float32 [65536, 8], P(('dp', 'expert'))
- d_gate_w: bfloat16 [3584, 8192], P('dp', 'expert')
- d_up_w: bfloat16 [3584, 8192], P('dp', 'expert')
- d_down_w: bfloat16 [3584, 8192], P('dp', 'expert')
Inputs may be any that keep to these rules, and one draw needn't show every extreme that they name: `route_ids`: each token names 8 different experts; the experts in flight are 0 to 7. Among the tokens of one device (aligned blocks of 128 tokens) each expert in flight is named by at most 6 tokens, and in every draw one expert in flight is named by exactly 6 tokens in every block.
All inputs are finite; a program needn't handle non-finite values.
Results may differ from a plain program's by a relative error of at most 0.017.
Values may be sent and summed in bfloat16 or wider, within the bound.
A program may use at most 64 MiB of HBM per device.

v0:
```python
import jax
import jax.numpy as jnp
from jax import lax
from jax.sharding import PartitionSpec as P

TOP = 8
SLICES = 8
CAP = 6


def shards(tokens, cotangent, route_ids, route_gates, gate_w, up_w, down_w):
    owners = lax.axis_size("expert")
    groups = owners // SLICES
    tok_rows = tokens.shape[0]
    routes = tok_rows * TOP
    flat_ids = route_ids.reshape(routes)
    matched = (flat_ids[:, None] == jnp.arange(groups, dtype=jnp.int32)[None, :]).astype(jnp.int32)
    slot_index = jnp.cumsum(matched, axis=0) - 1
    chosen = (matched[:, :, None] == 1) & (
        slot_index[:, :, None] == jnp.arange(CAP, dtype=jnp.int32)[None, None, :]
    )
    select = jnp.transpose(chosen, (1, 2, 0)).reshape(groups * CAP, routes).astype(jnp.float32)
    tok_select = jnp.sum(select.reshape(groups * CAP, tok_rows, TOP), axis=2)
    slot_gate = jnp.sum(select * route_gates.reshape(routes)[None, :], axis=1)
    pick_rows = tok_select.astype(jnp.bfloat16)
    token_slots = jnp.dot(pick_rows, tokens, preferred_element_type=jnp.float32).astype(
        jnp.bfloat16
    )
    cotangent_slots = jnp.dot(pick_rows, cotangent, preferred_element_type=jnp.float32).astype(
        jnp.bfloat16
    )
    scaled_slots = (slot_gate[:, None] * cotangent_slots.astype(jnp.float32)).astype(jnp.bfloat16)

    def spread(slot_rows):
        width = slot_rows.shape[1]
        grouped = slot_rows.reshape(groups, 1, CAP, width)
        return jnp.broadcast_to(grouped, (groups, SLICES, CAP, width)).reshape(owners * CAP, width)

    w_gate, w_up, w_down = (
        lax.all_gather(gate_w, "dp", axis=0, tiled=True),
        lax.all_gather(up_w, "dp", axis=0, tiled=True),
        lax.all_gather(down_w, "dp", axis=0, tiled=True),
    )
    token_rows = lax.all_to_all(
        spread(token_slots), "expert", split_axis=0, concat_axis=0, tiled=True
    )
    gate_pre = jnp.dot(token_rows, w_gate, preferred_element_type=jnp.float32)
    up_pre = jnp.dot(token_rows, w_up, preferred_element_type=jnp.float32)
    sigmoid_gate = jax.nn.sigmoid(gate_pre)
    active = gate_pre * sigmoid_gate
    hidden = (active * up_pre).astype(jnp.bfloat16)
    contract_cols = (((1,), (1,)), ((), ()))
    out_part = lax.dot_general(
        hidden, w_down, contract_cols, preferred_element_type=jnp.float32
    ).astype(jnp.bfloat16)
    out_back = lax.all_to_all(out_part, "expert", split_axis=0, concat_axis=0, tiled=True)
    scaled_rows = lax.all_to_all(
        spread(scaled_slots), "expert", split_axis=0, concat_axis=0, tiled=True
    )
    d_hidden = jnp.dot(scaled_rows, w_down, preferred_element_type=jnp.float32)
    d_gate_pre = (
        d_hidden * up_pre * sigmoid_gate * (1.0 + gate_pre * (1.0 - sigmoid_gate))
    ).astype(jnp.bfloat16)
    d_up_pre = (d_hidden * active).astype(jnp.bfloat16)
    dx_part = lax.dot_general(d_gate_pre, w_gate, contract_cols, preferred_element_type=jnp.float32)
    dx_part = (
        dx_part + lax.dot_general(d_up_pre, w_up, contract_cols, preferred_element_type=jnp.float32)
    ).astype(jnp.bfloat16)
    contract_rows = (((0,), (0,)), ((), ()))
    gate_term = lax.dot_general(
        token_rows, d_gate_pre, contract_rows, preferred_element_type=jnp.float32
    )
    up_term = lax.dot_general(
        token_rows, d_up_pre, contract_rows, preferred_element_type=jnp.float32
    )
    down_term = lax.dot_general(
        scaled_rows, hidden, contract_rows, preferred_element_type=jnp.float32
    )
    summed_grads = lax.psum_scatter(
        jnp.concatenate([gate_term, up_term, down_term], axis=1).astype(jnp.bfloat16),
        "dp",
        scatter_dimension=0,
        tiled=True,
    ).astype(jnp.float32)
    hidden_cols = gate_w.shape[1]
    d_gate_w = summed_grads[:, :hidden_cols].astype(jnp.bfloat16)
    d_up_w = summed_grads[:, hidden_cols : 2 * hidden_cols].astype(jnp.bfloat16)
    d_down_w = summed_grads[:, 2 * hidden_cols :].astype(jnp.bfloat16)
    dx_back = lax.all_to_all(dx_part, "expert", split_axis=0, concat_axis=0, tiled=True)
    member_wide = spread(tok_select)
    weighted_wide = spread(tok_select * slot_gate[:, None])
    weight_high = weighted_wide.astype(jnp.bfloat16)
    weight_low = (weighted_wide - weight_high.astype(jnp.float32)).astype(jnp.bfloat16)
    moe_sum = lax.dot_general(
        weight_high, out_back, contract_rows, preferred_element_type=jnp.float32
    )
    moe_sum = moe_sum + lax.dot_general(
        weight_low, out_back, contract_rows, preferred_element_type=jnp.float32
    )
    moe_out = moe_sum.astype(jnp.bfloat16)
    d_tokens = lax.dot_general(
        member_wide.astype(jnp.bfloat16), dx_back, contract_rows, preferred_element_type=jnp.float32
    ).astype(jnp.bfloat16)
    inner = lax.dot_general(cotangent, out_back, contract_cols, preferred_element_type=jnp.float32)
    wide_grad = jnp.sum(inner * jnp.transpose(member_wide), axis=0)
    slot_grad = jnp.sum(wide_grad.reshape(groups, SLICES, CAP), axis=1).reshape(groups * CAP)
    d_gates = jnp.sum(slot_grad[:, None] * select, axis=0).reshape(tok_rows, TOP)
    return (moe_out, d_tokens, d_gates, d_gate_w, d_up_w, d_down_w)


def solution(mesh):
    return jax.shard_map(
        shards,
        mesh=mesh,
        in_specs=(
            P(("dp", "expert"), None),
            P(("dp", "expert"), None),
            P(("dp", "expert"), None),
            P(("dp", "expert"), None),
            P("dp", "expert"),
            P("dp", "expert"),
            P("dp", "expert"),
        ),
        out_specs=(
            P(("dp", "expert"), None),
            P(("dp", "expert"), None),
            P(("dp", "expert"), None),
            P("dp", "expert"),
            P("dp", "expert"),
            P("dp", "expert"),
        ),
        check_vma=False,
    )
```

profile of v0, /device:TPU:1, one launch (start us, length us, event | category | flops | bytes accessed | tf_op | source)
XLA Modules:
  0.0 461.0 jit_solution(1026153735217437292)
XLA Ops:
  13.2 3.4 eq.81
  16.6 2.9 convert_reduce_fusion
  22.1 12.0 %all-to-all-start = ((bf16[64,6,3584]{2,1,0:T(8,128)(2,1)}), bf16[64,6,3584]{2,1,0:T(8,128)(2,1)}, u32[]{:S(2)}, u32[]{:S(2)}) async-start(bf16[64,6,3584]{2,1,0:T(8,128)(2,1)} %bitcast.37), calls=%async_computation | async-start | bytes 7340032 | tf_op jit(solution)/shard_map/all_to_all | solution.py:44
  34.0 29.5 %all_gather.9 = bf16[3584,128]{1,0:T(8,128)(2,1)S(1)} all-gather(bf16[448,128]{1,0:T(8,128)(2,1)S(1)} %copy-done.10), channel_id=1, replica_groups=mesh['dp'=8,'expert'=64] {'dp'}, dimensions={0}, use_global_device_ids=true | all-gather | bytes 1032192 | tf_op jit(solution)/shard_map/all_gather | solution.py:40
  63.6 22.6 %all_gather.10 = bf16[3584,128]{1,0:T(8,128)(2,1)S(1)} all-gather(bf16[448,128]{1,0:T(8,128)(2,1)S(1)} %copy-done.11), channel_id=1, replica_groups=mesh['dp'=8,'expert'=64] {'dp'}, dimensions={0}, use_global_device_ids=true | all-gather | bytes 1032192 | tf_op jit(solution)/shard_map/all_gather | solution.py:41
  86.2 24.5 %all_gather.11 = bf16[3584,128]{1,0:T(8,128)(2,1)} all-gather(bf16[448,128]{1,0:T(8,128)(2,1)S(1)} %copy-done.12), channel_id=1, replica_groups=mesh['dp'=8,'expert'=64] {'dp'}, dimensions={0}, use_global_device_ids=true | all-gather | bytes 1032192 | tf_op jit(solution)/shard_map/all_gather | solution.py:42
  110.7 7.2 %all-to-all-done = bf16[64,6,3584]{2,1,0:T(8,128)(2,1)} async-done(((bf16[64,6,3584]{2,1,0:T(8,128)(2,1)}), bf16[64,6,3584]{2,1,0:T(8,128)(2,1)}, u32[]{:S(2)}, u32[]{:S(2)}) %all-to-all-start) | async-done | bytes 2752544 | tf_op jit(solution)/shard_map/all_to_all | solution.py:44
  117.9 5.4 %all_to_all.34 = bf16[384,3584]{1,0:T(8,128)(2,1)} reshape(bf16[64,6,3584]{2,1,0:T(8,128)(2,1)} %all-to-all-done) | data formatting | bytes 5505024 | tf_op jit(solution)/shard_map/all_to_all | solution.py:44
  123.4 2.8 fusion.12
  129.8 5.4 %all_to_all.35 = bf16[64,6,3584]{2,1,0:T(8,128)(2,1)} reshape(bf16[384,3584]{1,0:T(8,128)(2,1)} %convolution_convert_fusion) | data formatting | bytes 5505024 | tf_op jit(solution)/shard_map/all_to_all | solution.py:56
  135.2 13.6 %all-to-all-start.1 = ((bf16[64,6,3584]{2,1,0:T(8,128)(2,1)}), bf16[64,6,3584]{2,1,0:T(8,128)(2,1)}, u32[]{:S(2)}, u32[]{:S(2)}) async-start(bf16[64,6,3584]{2,1,0:T(8,128)(2,1)} %all_to_all.35), calls=%async_computation.1 | async-start | bytes 7340032 | tf_op jit(solution)/shard_map/all_to_all | solution.py:56
  149.2 83.3 %all-to-all-done.1 = bf16[64,6,3584]{2,1,0:T(8,128)(2,1)} async-done(((bf16[64,6,3584]{2,1,0:T(8,128)(2,1)}), bf16[64,6,3584]{2,1,0:T(8,128)(2,1)}, u32[]{:S(2)}, u32[]{:S(2)}) %all-to-all-start.1) | async-done | bytes 2752544 | tf_op jit(solution)/shard_map/all_to_all | solution.py:56
  232.5 5.5 %all_to_all.37 = bf16[384,3584]{1,0:T(8,128)(2,1)} reshape(bf16[64,6,3584]{2,1,0:T(8,128)(2,1)} %all-to-all-done.1) | data formatting | bytes 5505024 | tf_op jit(solution)/shard_map/all_to_all | solution.py:56
  238.0 2.7 fusion.5
  241.9 90.5 %all_to_all.48 = bf16[64,6,3584]{2,1,0:T(8,128)(2,1)} all-to-all(bf16[64,6,3584]{2,1,0:T(8,128)(2,1)S(1)} %bitcast.38), channel_id=1, replica_groups=mesh['dp'=8,'expert'=64] {'expert'}, dimensions={0} | all-to-all | bytes 5505024 | tf_op jit(solution)/shard_map/all_to_all | solution.py:57
  332.4 5.5 %all_to_all.40 = bf16[384,3584]{1,0:T(8,128)(2,1)} reshape(bf16[64,6,3584]{2,1,0:T(8,128)(2,1)} %all_to_all.48) | data formatting | bytes 5505024 | tf_op jit(solution)/shard_map/all_to_all | solution.py:57
  337.9 2.6 convolution_convert_fusion.1
  347.7 5.4 %all_to_all.41 = bf16[64,6,3584]{2,1,0:T(8,128)(2,1)} reshape(bf16[384,3584]{1,0:T(8,128)(2,1)} %fusion) | data formatting | bytes 5505024 | tf_op jit(solution)/shard_map/all_to_all | solution.py:89
  353.1 6.5 %all-to-all-start.3 = ((bf16[64,6,3584]{2,1,0:T(8,128)(2,1)}), bf16[64,6,3584]{2,1,0:T(8,128)(2,1)}, u32[]{:S(2)}, u32[]{:S(2)}) async-start(bf16[64,6,3584]{2,1,0:T(8,128)(2,1)} %all_to_all.41), calls=%async_computation.3 | async-start | bytes 7340032 | tf_op jit(solution)/shard_map/all_to_all | solution.py:89
  361.4 4.5 copy.35
  369.4 3.4 fusion.1
  372.8 70.6 %all-to-all-done.3 = bf16[64,6,3584]{2,1,0:T(8,128)(2,1)} async-done(((bf16[64,6,3584]{2,1,0:T(8,128)(2,1)}), bf16[64,6,3584]{2,1,0:T(8,128)(2,1)}, u32[]{:S(2)}, u32[]{:S(2)}) %all-to-all-start.3) | async-done | bytes 2752544 | tf_op jit(solution)/shard_map/all_to_all | solution.py:89
  443.4 5.6 %all_to_all.43 = bf16[384,3584]{1,0:T(8,128)(2,1)} reshape(bf16[64,6,3584]{2,1,0:T(8,128)(2,1)} %all-to-all-done.3) | data formatting | bytes 5505024 | tf_op jit(solution)/shard_map/all_to_all | solution.py:89
  449.0 3.4 convolution_convert_fusion.4
  (81 shorter events, 27.6 us)
Async XLA Ops:
  7.2 230.9 %copy-start = (bf16[128,3584]{1,0:T(8,128)(2,1)S(1)}, bf16[128,3584]{1,0:T(8,128)(2,1)}, u32[]{:S(2)}) copy-start(bf16[128,3584]{1,0:T(8,128)(2,1)} %param.8) | copy-start | bytes 2752516
  16.6 2.9 copy-start.9
  22.0 12.0 %copy-start.10 = (bf16[448,128]{1,0:T(8,128)(2,1)S(1)}, bf16[448,128]{1,0:T(8,128)(2,1)}, u32[]{:S(2)}) copy-start(bf16[448,128]{1,0:T(8,128)(2,1)} %param.11) | copy-start | bytes 344068
  22.0 41.5 %copy-start.11 = (bf16[448,128]{1,0:T(8,128)(2,1)S(1)}, bf16[448,128]{1,0:T(8,128)(2,1)}, u32[]{:S(2)}) copy-start(bf16[448,128]{1,0:T(8,128)(2,1)} %param.12) | copy-start | bytes 344068
  22.1 64.1 %copy-start.12 = (bf16[448,128]{1,0:T(8,128)(2,1)S(1)}, bf16[448,128]{1,0:T(8,128)(2,1)}, u32[]{:S(2)}) copy-start(bf16[448,128]{1,0:T(8,128)(2,1)} %param.13) | copy-start | bytes 344068
  22.1 95.9 %all-to-all-start = ((bf16[64,6,3584]{2,1,0:T(8,128)(2,1)}), bf16[64,6,3584]{2,1,0:T(8,128)(2,1)}, u32[]{:S(2)}, u32[]{:S(2)}) async-start(bf16[64,6,3584]{2,1,0:T(8,128)(2,1)} %bitcast.37), calls=%async_computation | async-start | bytes 7340032 | tf_op jit(solution)/shard_map/all_to_all | solution.py:44
  86.2 40.0 %copy-start.5 = (bf16[3584,128]{1,0:T(8,128)(2,1)}, bf16[3584,128]{1,0:T(8,128)(2,1)S(1)}, u32[]{:S(2)}) copy-start(bf16[3584,128]{1,0:T(8,128)(2,1)S(1)} %all_gather.10) | copy-start | bytes 2752516
  123.4 2.8 copy-start.2
  126.2 1.2 copy-start.7
  135.2 13.6 %copy-start.13 = (f32[128,8]{0,1:T(8,128)S(1)}, f32[128,8]{0,1:T(8,128)}, u32[]{:S(2)}) copy-start(f32[128,8]{0,1:T(8,128)} %param.10) | copy-start | bytes 12292
  135.2 97.3 %all-to-all-start.1 = ((bf16[64,6,3584]{2,1,0:T(8,128)(2,1)}), bf16[64,6,3584]{2,1,0:T(8,128)(2,1)}, u32[]{:S(2)}, u32[]{:S(2)}) async-start(bf16[64,6,3584]{2,1,0:T(8,128)(2,1)} %all_to_all.35), calls=%async_computation.1 | async-start | bytes 7340032 | tf_op jit(solution)/shard_map/all_to_all | solution.py:56
  337.9 2.6 copy-start.4
  337.9 2.8 copy-start.8
  340.7 1.8 copy-start.3
  344.1 1.2 copy-start.6
  353.1 90.3 %all-to-all-start.3 = ((bf16[64,6,3584]{2,1,0:T(8,128)(2,1)}), bf16[64,6,3584]{2,1,0:T(8,128)(2,1)}, u32[]{:S(2)}, u32[]{:S(2)}) async-start(bf16[64,6,3584]{2,1,0:T(8,128)(2,1)} %all_to_all.41), calls=%async_computation.3 | async-start | bytes 7340032 | tf_op jit(solution)/shard_map/all_to_all | solution.py:89
  359.6 92.7 %reduce-scatter.4.cloned.1.call-start = ((), (), s32[]{:S(2)}) async-start(), calls=%async_computation.5 | async-start | bytes 3096576
  443.4 10.7 %copy-start.1 = (bf16[128,3584]{1,0:T(8,128)(2,1)S(1)}, bf16[128,3584]{1,0:T(8,128)(2,1)}, u32[]{:S(2)}) copy-start(bf16[128,3584]{1,0:T(8,128)(2,1)} %param.8) | copy-start | bytes 2752516
Sparse Core Ops, SparseCore 0:
  366.0 43.2 reduce-scatter.3
where the time goes:
time: 463 us; the launch traced here: 461 us
  blocking collectives  167 us (36%)
  waiting for transfers between devices  161 us (35%)
  local copies, waits for them, and re-layouts  51.9 us (11%)
  starting transfers between devices  32.1 us (7%)
  matrix products  26.8 us (6%)
  between operations  14.4 us (3%)
  other arithmetic  7.41 us (2%)
    all_to_all x1, blocking collectives, shards(): lax.all_to_all(spread(scaled_slots), 'expert', split_axis=0, concat_axis=...  90.5 us
    all_to_all x1, waiting for transfers between devices, shards(): lax.all_to_all(out_part, 'expert', split_axis=0, concat_axis=0, tiled=True)  83.3 us
    all_to_all x1, waiting for transfers between devices, shards(): lax.all_to_all(dx_part, 'expert', split_axis=0, concat_axis=0, tiled=True)  70.6 us
    all_gather x1, blocking collectives, shards(): lax.all_gather(gate_w, 'dp', axis=0, tiled=True)  29.5 us
    all_gather x1, blocking collectives, shards(): lax.all_gather(down_w, 'dp', axis=0, tiled=True)  24.5 us
    all_gather x1, blocking collectives, shards(): lax.all_gather(up_w, 'dp', axis=0, tiled=True)  22.6 us
    all_to_all x1, starting transfers between devices, shards(): lax.all_to_all(out_part, 'expert', split_axis=0, concat_axis=0, tiled=True)  13.6 us
    all_to_all x1, starting transfers between devices, shards(): lax.all_to_all(spread(token_slots), 'expert', split_axis=0, concat_axis=0...  12 us
  transfers between devices with their start and end apart: 4, of which 3 were waited for; matrix products, arithmetic and copies ran while one was open for 4% of the time, Pallas kernels for 0%

commit v1 on v0

v1 whole, which is shorter than its diff:
```python
import jax
import jax.numpy as jnp
from jax import lax
from jax.sharding import Mesh, PartitionSpec as P

SLICES = 8
CAP = 6
PAD = 8
BF = jnp.bfloat16
F32 = jnp.float32
CONTRACT_COLS = (((1,), (1,)), ((), ()))
CONTRACT_ROWS = (((0,), (0,)), ((), ()))


def dot(a, b, dims=(((1,), (0,)), ((), ()))):
    return lax.dot_general(a, b, dims, preferred_element_type=F32)


def routing(route_ids, route_gates, groups):
    tok_rows = route_ids.shape[0]
    experts = jnp.arange(groups, dtype=jnp.int32)
    match = route_ids[:, :, None] == experts[None, None, :]
    member = jnp.sum(match.astype(F32), axis=1)
    gate = jnp.sum(jnp.where(match, route_gates[:, :, None], 0.0), axis=1)
    row = lax.broadcasted_iota(jnp.int32, (tok_rows, tok_rows), 0)
    col = lax.broadcasted_iota(jnp.int32, (tok_rows, tok_rows), 1)
    before = (col < row).astype(BF)
    slot = dot(before, member.astype(BF))
    return match, member, gate, slot


def shards(tokens, cotangent, route_ids, route_gates, gate_w, up_w, down_w):
    groups = lax.axis_size("y")
    width = tokens.shape[1]
    tok_rows = tokens.shape[0]
    hid = gate_w.shape[1]
    match, member, gate, slot = routing(route_ids, route_gates, groups)
    wide = (jnp.where(member > 0.5, slot, -1.0).T)[:, None, :]
    sel = (wide == jnp.arange(PAD, dtype=F32)[None, :, None]).astype(F32)
    gates_t = gate.T[:, None, :]
    slot_gate = jnp.sum(sel * gates_t, axis=2)
    pick = sel.reshape(groups * PAD, tok_rows).astype(BF)
    token_slots = dot(pick, tokens).astype(BF)
    cot_slots = dot(pick, cotangent)
    scaled_slots = (slot_gate.reshape(groups * PAD, 1) * cot_slots).astype(BF)
    send = jnp.concatenate(
        [token_slots.reshape(groups, PAD, width), scaled_slots.reshape(groups, PAD, width)], axis=1
    )
    w_all = lax.all_gather(
        jnp.concatenate([gate_w, up_w, down_w], axis=1), "dp", axis=0, tiled=True
    )
    w_gate, w_up, w_down = w_all[:, :hid], w_all[:, hid : 2 * hid], w_all[:, 2 * hid :]
    came = lax.all_to_all(send, "y", split_axis=0, concat_axis=0, tiled=True)
    rows = groups * CAP
    out_row = lax.broadcasted_iota(jnp.int32, (2 * rows, groups * 2 * PAD), 0)
    in_row = lax.broadcasted_iota(jnp.int32, (2 * rows, groups * 2 * PAD), 1)
    kind = (out_row >= rows).astype(jnp.int32)
    local = out_row - kind * rows
    wanted = (local // CAP) * (2 * PAD) + kind * PAD + local % CAP
    squeeze = (in_row == wanted).astype(BF)
    compact = dot(squeeze, came.reshape(groups * 2 * PAD, width)).astype(BF)
    both = lax.all_gather(compact, ("x", "c"), axis=0, tiled=False)
    n_slices = both.shape[0]
    token_rows = both[:, :rows].reshape(n_slices * rows, width)
    scaled_rows = both[:, rows:].reshape(n_slices * rows, width)

    gate_pre = dot(token_rows, w_gate)
    up_pre = dot(token_rows, w_up)
    sig = jax.nn.sigmoid(gate_pre)
    active = gate_pre * sig
    hidden = (active * up_pre).astype(BF)
    d_hidden = dot(scaled_rows, w_down)
    d_gate_pre = (d_hidden * up_pre * sig * (1.0 + gate_pre * (1.0 - sig))).astype(BF)
    d_up_pre = (d_hidden * active).astype(BF)
    out_part = dot(hidden, w_down, CONTRACT_COLS).astype(BF)
    dx_part = (
        dot(d_gate_pre, w_gate, CONTRACT_COLS) + dot(d_up_pre, w_up, CONTRACT_COLS)
    ).astype(BF)
    parts = jnp.concatenate(
        [out_part.reshape(n_slices, rows, width), dx_part.reshape(n_slices, rows, width)], axis=1
    ).reshape(n_slices * 2 * rows, width)
    summed = lax.psum_scatter(parts, ("x", "c"), scatter_dimension=0, tiled=True)
    grads = jnp.concatenate(
        [
            dot(token_rows, d_gate_pre, CONTRACT_ROWS),
            dot(token_rows, d_up_pre, CONTRACT_ROWS),
            dot(scaled_rows, hidden, CONTRACT_ROWS),
        ],
        axis=1,
    ).astype(BF)
    grads = lax.psum_scatter(grads, "dp", scatter_dimension=0, tiled=True)
    back = dot(squeeze, summed, CONTRACT_ROWS).astype(BF).reshape(groups, 2 * PAD, width)
    back = lax.all_to_all(back, "y", split_axis=0, concat_axis=0, tiled=True)
    back = back.reshape(groups * 2 * PAD, width)

    zero = jnp.zeros_like(sel)
    member_out = jnp.concatenate([sel, zero], axis=1).reshape(groups * 2 * PAD, tok_rows)
    member_dx = jnp.concatenate([zero, sel], axis=1).reshape(groups * 2 * PAD, tok_rows)
    weight = jnp.concatenate([sel * gates_t, zero], axis=1).reshape(groups * 2 * PAD, tok_rows)
    high = weight.astype(BF)
    low = (weight - high.astype(F32)).astype(BF)
    moe_out = (dot(high, back, CONTRACT_ROWS) + dot(low, back, CONTRACT_ROWS)).astype(BF)
    d_tokens = dot(member_dx.astype(BF), back, CONTRACT_ROWS).astype(BF)
    inner = dot(back, cotangent, CONTRACT_COLS) * member_out
    by_expert = jnp.sum(inner.reshape(groups, 2 * PAD, tok_rows), axis=1).T
    d_gates = jnp.sum(jnp.where(match, by_expert[:, None, :], 0.0), axis=2)
    return (
        moe_out,
        d_tokens,
        d_gates,
        grads[:, :hid],
        grads[:, hid : 2 * hid],
        grads[:, 2 * hid :],
    )


def solution(mesh):
    dp, owners = mesh.devices.shape
    y = owners // SLICES
    grid = Mesh(mesh.devices.reshape(dp, y, SLICES // 2, 2), ("dp", "y", "x", "c"))
    rows = P(("dp", "y", "x", "c"), None)
    cols = P("dp", ("y", "x", "c"))
    return jax.shard_map(
        shards,
        mesh=grid,
        in_specs=(rows, rows, rows, rows, cols, cols, cols),
        out_specs=(rows, rows, rows, cols, cols, cols),
        check_vma=False,
    )
```

time: 463 us -> 256 us (0.55)
  blocking collectives: 167 us -> 0 us
  local copies, waits for them, and re-layouts: 51.9 us -> 12 us
  waiting for transfers between devices: 161 us -> 183 us
  starting transfers between devices: 32.1 us -> 14.2 us
  matrix products: 26.8 us -> 22.1 us
    all_to_all x3 -> x2, waiting for transfers between devices: 161 us -> 24.1 us  [the longest x1 24.1 us: shards(): came = lax.all_to_all(send, 'y', split_axis=0, concat_axis=0, tiled=True)]
    all_to_all x1 -> x0, blocking collectives: 90.5 us -> none  [shards(): lax.all_to_all(spread(scaled_slots), 'expert', split_axis=0, concat_axis=...]
    all_gather x0 -> x2, waiting for transfers between devices: none -> 84.7 us  [the longest x1 44 us: shards(): both = lax.all_gather(compact, ('x', 'c'), axis=0, tiled=False)]
    all_gather x3 -> x0, blocking collectives: 76.7 us -> none  [the longest x1 29.5 us: shards(): lax.all_gather(gate_w, 'dp', axis=0, tiled=True)]
    unnamed x2 -> x5, waiting for transfers between devices: 0.02 us -> 40.4 us
    reduce_scatter x0 -> x1, waiting for transfers between devices: none -> 33.8 us  [shards(): lax.psum_scatter(parts, ('x', 'c'), scatter_dimension=0, tiled=True)]
    all_to_all x6 -> x0, local copies, waits for them, and re-layouts: 32.8 us -> none  [the longest x2 11 us: shards(): lax.all_to_all(dx_part, 'expert', split_axis=0, concat_axis=0, tiled=True)]
    all_to_all x3 -> x2, starting transfers between devices: 32.1 us -> 14 us  [the longest x1 7.64 us: shards(): came = lax.all_to_all(send, 'y', split_axis=0, concat_axis=0, tiled=True)]
  transfers between devices with their start and end apart: 4 -> 6, of which waited for: 3 -> 5; matrix products, arithmetic and copies ran while one was open for 4% -> 8% of each run, Pallas kernels for 0% -> 0%
where the time goes in v1:
time: 256 us; the launch traced here: 253 us
  waiting for transfers between devices  183 us (71%)
  matrix products  22.1 us (9%)
  starting transfers between devices  14.2 us (6%)
  between operations  14 us (5%)
  local copies, waits for them, and re-layouts  12 us (5%)
  other arithmetic  7.87 us (3%)
    all_gather x1, waiting for transfers between devices, shards(): both = lax.all_gather(compact, ('x', 'c'), axis=0, tiled=False)  44 us
    all_gather x1, waiting for transfers between devices, shards(): lax.all_gather(jnp.concatenate([gate_w, up_w, down_w], axis=1), 'dp', axi...  40.7 us
    unnamed x5, waiting for transfers between devices  40.4 us
    reduce_scatter x1, waiting for transfers between devices, shards(): lax.psum_scatter(parts, ('x', 'c'), scatter_dimension=0, tiled=True)  33.8 us
    all_to_all x1, waiting for transfers between devices, shards(): came = lax.all_to_all(send, 'y', split_axis=0, concat_axis=0, tiled=True)  24.1 us
    dot_general x18, matrix products, dot(): return lax.dot_general(a, b, dims, preferred_element_type=F32)  22.1 us
    all_to_all x1, starting transfers between devices, shards(): came = lax.all_to_all(send, 'y', split_axis=0, concat_axis=0, tiled=True)  7.64 us
    all_to_all x1, starting transfers between devices, shards(): back = lax.all_to_all(back, 'y', split_axis=0, concat_axis=0, tiled=True)  6.39 us
  transfers between devices with their start and end apart: 6, of which 5 were waited for; matrix products, arithmetic and copies ran while one was open for 8% of the time, Pallas kernels for 0%

profile of v1, /device:TPU:1, one launch (start us, length us, event | category | flops | bytes accessed | tf_op | source)
XLA Modules:
  0.0 253.2 jit_solution(2671036714309216586)
XLA Ops:
  8.4 1.5 fusion.6
  10.3 1.0 pad_maximum_fusion.2
  11.3 7.6 %all-to-all-start = ((bf16[8,16,3584]{2,1,0:T(8,128)(2,1)}), bf16[8,16,3584]{2,1,0:T(8,128)(2,1)S(1)}, u32[]{:S(2)}, u32[]{:S(2)}) async-start(bf16[8,16,3584]{2,1,0:T(8,128)(2,1)} %pad_maximum_fusion.2), calls=%async_computation | async-start | bytes 1835008 | tf_op jit(solution)/shard_map/all_to_all | solution.py:53
  19.0 24.1 %all-to-all-done = bf16[8,16,3584]{2,1,0:T(8,128)(2,1)S(1)} async-done(((bf16[8,16,3584]{2,1,0:T(8,128)(2,1)}), bf16[8,16,3584]{2,1,0:T(8,128)(2,1)S(1)}, u32[]{:S(2)}, u32[]{:S(2)}) %all-to-all-start) | async-done | bytes 917536 | tf_op jit(solution)/shard_map/all_to_all | solution.py:53
  43.2 1.3 convolution_convert_fusion.5
  45.4 44.0 %all-gather.6.cloned.1.call-done = bf16[768,3584]{1,0:T(8,128)(2,1)} async-done(((bf16[96,3584]{1,0:T(8,128)(2,1)}), bf16[768,3584]{1,0:T(8,128)(2,1)}) %all-gather.6.cloned.1.call-update) | async-done | bytes 5505040 | tf_op jit(solution)/shard_map/all_gather | solution.py:62
  89.3 5.5 %fusion.33 = (bf16[8,48,3584]{2,1,0:T(8,128)(2,1)}, bf16[8,48,3584]{2,1,0:T(8,128)(2,1)}) fusion(bf16[8,96,3584]{2,1,0:T(8,128)(2,1)} %bitcast.70), kind=kLoop, calls=%fused_computation.75 | loop fusion | bytes 11010048 | tf_op jit(solution)/shard_map/slice | solution.py:65
  94.8 40.7 %all-gather.4.cloned.1.call-done = bf16[3584,384]{1,0:T(8,128)(2,1)} async-done(((bf16[448,384]{1,0:T(8,128)(2,1)}), bf16[3584,384]{1,0:T(8,128)(2,1)}) %all-gather.4.cloned.1.call-update) | async-done | bytes 2752528 | tf_op jit(solution)/shard_map/all_gather | solution.py:49
  135.5 3.0 %fusion.15 = f32[384,128]{1,0:T(8,128)S(1)} fusion(bf16[384,3584]{1,0:T(8,128)(2,1)} %bitcast.60, bf16[3584,384]{1,0:T(8,128)(2,1)} %all-gather.4.cloned.1.call-done), kind=kOutput, calls=%fused_computation.32 | convolution fusion | flops 352321536 | bytes 3866624 | tf_op jit(solution)/shard_map/dot_general | solution.py:16
  138.6 2.2 fusion.7
  140.8 0.9 multiply_convert_fusion.2
  141.7 0.9 fusion.13
  143.5 0.9 fusion
  144.3 2.8 %pad_maximum_fusion = bf16[8,96,3584]{2,1,0:T(8,128)(2,1)} fusion(bf16[8,48,3584]{2,1,0:T(8,128)(2,1)S(1)} %bitcast.69, bf16[8,48,3584]{2,1,0:T(8,128)(2,1)S(1)} %bitcast.68), kind=kLoop, calls=%fused_computation.3 | loop fusion | flops 11010048 | bytes 11010048 | tf_op jit(solution)/shard_map/concatenate | solution.py:79
  147.2 2.6 %convolution_convert_fusion.1 = bf16[3584,128]{0,1:T(8,128)(2,1)S(1)} fusion(bf16[384,3584]{1,0:T(8,128)(2,1)} %bitcast.66, bf16[384,128]{1,0:T(8,128)(2,1)S(1)} %get-tuple-element.28), kind=kOutput, calls=%fused_computation.10 | convolution fusion | flops 352780288 | bytes 3768320 | tf_op jit(solution)/shard_map/dot_general | solution.py:16
  151.2 1.8 pad_maximum_fusion.1
  153.0 4.5 %copy.27 = bf16[3584,384]{1,0:T(8,128)(2,1)} copy(bf16[3584,384]{0,1:T(8,128)(2,1)} %pad_maximum_fusion.1) | data formatting | bytes 5505024
  157.6 33.8 %reduce-scatter.5.cloned.1.call-done = bf16[96,3584]{1,0:T(8,128)(2,1)} async-done(((bf16[768,3584]{1,0:T(8,128)(2,1)}), bf16[96,3584]{1,0:T(8,128)(2,1)}) %reduce-scatter.5.cloned.1.call-update) | async-done | bytes 688144 | tf_op jit(solution)/shard_map/reduce_scatter | solution.py:82
  191.4 2.6 %convolution_convert_fusion.4 = bf16[128,3584]{1,0:T(8,128)(2,1)} fusion(bf16[96,3584]{1,0:T(8,128)(2,1)} %reduce-scatter.5.cloned.1.call-done, s32[96]{0:T(128)S(1)} %broadcast_remainder_fusion, s32[96]{0:T(128)S(1)} %get-tuple-element.42, s32[96]{0:T(128)S(1)} %get-tuple-element.40, s32[96]{0:T(128)S(1)} %get-tuple-element.43, ...), kind=kOutput, calls=%fused_computation.13 | convolution fusion | flops 88612864 | bytes 1607744 | tf_op jit(solution)/shard_map/dot_general | solution.py:16
  194.0 6.4 %all-to-all-start.1 = ((bf16[8,16,3584]{2,1,0:T(8,128)(2,1)}), bf16[8,16,3584]{2,1,0:T(8,128)(2,1)S(1)}, u32[]{:S(2)}, u32[]{:S(2)}) async-start(bf16[8,16,3584]{2,1,0:T(8,128)(2,1)} %bitcast.12), calls=%async_computation.2 | async-start | bytes 1835008 | tf_op jit(solution)/shard_map/all_to_all | solution.py:93
  200.4 40.4 %reduce-scatter.7.cloned.1.call-done = bf16[448,384]{1,0:T(8,128)(2,1)} async-done(((bf16[3584,384]{1,0:T(8,128)(2,1)}), bf16[448,384]{1,0:T(8,128)(2,1)}) %reduce-scatter.7.cloned.1.call-update) | async-done | bytes 344080
  240.8 1.7 fusion.34
  244.0 1.3 fusion.2
  245.3 1.3 fusion.3
  (47 shorter events, 6.4 us)
Async XLA Ops:
  7.2 2.8 %copy-start = (bf16[128,3584]{1,0:T(8,128)(2,1)S(1)}, bf16[128,3584]{1,0:T(8,128)(2,1)}, u32[]{:S(2)}) copy-start(bf16[128,3584]{1,0:T(8,128)(2,1)} %param.8) | copy-start | bytes 2752516
  10.3 34.2 %copy-start.5 = (bf16[448,128]{1,0:T(8,128)(2,1)S(1)}, bf16[448,128]{1,0:T(8,128)(2,1)}, u32[]{:S(2)}) copy-start(bf16[448,128]{1,0:T(8,128)(2,1)} %param.13) | copy-start | bytes 344068
  10.3 34.2 %copy-start.6 = (bf16[448,128]{1,0:T(8,128)(2,1)S(1)}, bf16[448,128]{1,0:T(8,128)(2,1)}, u32[]{:S(2)}) copy-start(bf16[448,128]{1,0:T(8,128)(2,1)} %param.12) | copy-start | bytes 344068
  10.3 34.2 %copy-start.7 = (bf16[448,128]{1,0:T(8,128)(2,1)S(1)}, bf16[448,128]{1,0:T(8,128)(2,1)}, u32[]{:S(2)}) copy-start(bf16[448,128]{1,0:T(8,128)(2,1)} %param.11) | copy-start | bytes 344068
  11.3 31.9 %all-to-all-start = ((bf16[8,16,3584]{2,1,0:T(8,128)(2,1)}), bf16[8,16,3584]{2,1,0:T(8,128)(2,1)S(1)}, u32[]{:S(2)}, u32[]{:S(2)}) async-start(bf16[8,16,3584]{2,1,0:T(8,128)(2,1)} %pad_maximum_fusion.2), calls=%async_computation | async-start | bytes 1835008 | tf_op jit(solution)/shard_map/all_to_all | solution.py:53
  18.9 70.4 %all-gather.6.cloned.1.call-start = ((), (), s32[]{:S(2)}) async-start(), calls=%async_computation.6 | async-start | bytes 6193152 | tf_op jit(solution)/shard_map/all_gather | solution.py:62
  44.5 91.1 %all-gather.4.cloned.1.call-start = ((), (), s32[]{:S(2)}) async-start(), calls=%async_computation.4 | async-start | bytes 3096576 | tf_op jit(solution)/shard_map/all_gather | solution.py:49
  45.3 146.0 %reduce-scatter.5.cloned.1.call-start = ((), (), s32[]{:S(2)}) async-start(), calls=%async_computation.5 | async-start | bytes 6193152 | tf_op jit(solution)/shard_map/reduce_scatter | solution.py:82
  135.5 3.0 %copy-start.3 = (bf16[8,48,3584]{2,1,0:T(8,128)(2,1)S(1)}, bf16[8,48,3584]{2,1,0:T(8,128)(2,1)}, u32[]{:S(2)}) copy-start(bf16[8,48,3584]{2,1,0:T(8,128)(2,1)} %get-tuple-element.26) | copy-start | bytes 8257540
  135.5 5.3 %copy-start.4 = (bf16[3584,384]{1,0:T(8,128)(2,1)S(1)}, bf16[3584,384]{1,0:T(8,128)(2,1)}, u32[]{:S(2)}) copy-start(bf16[3584,384]{1,0:T(8,128)(2,1)} %all-gather.4.cloned.1.call-done) | copy-start | bytes 8257540
  138.6 2.2 copy-start.1
  147.1 93.6 %reduce-scatter.7.cloned.1.call-start = ((), (), s32[]{:S(2)}) async-start(), calls=%async_computation.7 | async-start | bytes 3096576
  147.2 2.6 %copy-start.2 = (bf16[8,48,3584]{2,1,0:T(8,128)(2,1)S(1)}, bf16[8,48,3584]{2,1,0:T(8,128)(2,1)}, u32[]{:S(2)}) copy-start(bf16[8,48,3584]{2,1,0:T(8,128)(2,1)} %get-tuple-element.27) | copy-start | bytes 8257540
  157.6 85.3 %copy-start.8 = (s32[128,8]{0,1:T(8,128)S(1)}, s32[128,8]{0,1:T(8,128)}, u32[]{:S(2)}) copy-start(s32[128,8]{0,1:T(8,128)} %param.9) | copy-start | bytes 12292
  194.0 48.5 %all-to-all-start.1 = ((bf16[8,16,3584]{2,1,0:T(8,128)(2,1)}), bf16[8,16,3584]{2,1,0:T(8,128)(2,1)S(1)}, u32[]{:S(2)}, u32[]{:S(2)}) async-start(bf16[8,16,3584]{2,1,0:T(8,128)(2,1)} %bitcast.12), calls=%async_computation.2 | async-start | bytes 1835008 | tf_op jit(solution)/shard_map/all_to_all | solution.py:93
Sparse Core Ops, SparseCore 0:
  44.6 44.7 all-gather.5
  92.0 43.4 all-gather.3
  147.3 44.0 reduce-scatter.4
  194.1 46.6 reduce-scatter.6

commit v2 on v1

--- a/solution.py
+++ b/solution.py
@@ -1,6 +1,11 @@
+import functools
+
 import jax
 import jax.numpy as jnp
+import numpy as np
 from jax import lax
+from jax.experimental import pallas as pl
+from jax.experimental.pallas import tpu as pltpu
 from jax.sharding import Mesh, PartitionSpec as P
 
 SLICES = 8
@@ -14,6 +19,160 @@
 
 def dot(a, b, dims=(((1,), (0,)), ((), ()))):
     return lax.dot_general(a, b, dims, preferred_element_type=F32)
+
+
+def squeeze_matrix(groups):
+    rows = groups * CAP
+    out_row = np.arange(2 * rows)
+    kind = out_row // rows
+    local = out_row % rows
+    wanted = (local // CAP) * (2 * PAD) + kind * PAD + local % CAP
+    return jnp.asarray(np.arange(groups * 2 * PAD)[None, :] == wanted[:, None], BF)
+
+
+def push(src, dst, send, recv, where):
+    return pltpu.make_async_remote_copy(
+        src_ref=src, dst_ref=dst, send_sem=send, recv_sem=recv,
+        device_id=where, device_id_type=pl.DeviceIdType.MESH,
+    )
+
+
+RIGHT, LEFT, PAIR, FAR, PAIR_L, PAIR_R, PAIR_FAR = range(7)
+
+
+def gather_kernel(nz, ny, nx, chunks, send_ref, w_ref, squeeze_ref, tok_ref, scl_ref, wall_ref,
+                  came, y_send, y_recv, x_send, x_recv, z_send, z_recv):
+    z, y, x, c = (lax.axis_index(n) for n in ("dp", "y", "x", "c"))
+    width = send_ref.shape[2]
+    step = width // chunks
+    half = w_ref.shape[0] // 2
+    x_right, x_left, x_far = (lax.rem(x + k, nx) for k in (1, nx - 1, 2))
+    z_right, z_left = lax.rem(z + 1, nz), lax.rem(z + nz - 1, nz)
+    mine = x * 2 + c
+    outs = (tok_ref, scl_ref)
+    rows = tok_ref.shape[1]
+    peers = [{"y": lax.rem(y + k, ny)} for k in range(1, ny)]
+    peers += [{"x": x_right}, {"x": x_left}, {"c": 1 - c}, {"dp": z_right}, {"dp": z_left}]
+    barrier = pltpu.get_barrier_semaphore()
+    for peer in peers:
+        pl.semaphore_signal(barrier, inc=1, device_id=peer, device_id_type=pl.DeviceIdType.MESH)
+    pl.semaphore_wait(barrier, len(peers))
+
+    def z_copy(way, s):
+        source = lax.rem(z + (nz - s if way == 0 else s), nz)
+        part = pl.ds(0, 2 * half) if s < nz // 2 - 1 else pl.ds(way * half, half)
+        src = w_ref if s == 0 else wall_ref.at[source]
+        return push(src.at[part, :], wall_ref.at[source, part, :], z_send.at[way, s],
+                    z_recv.at[way, s], {"dp": z_right if way == 0 else z_left})
+
+    def y_copy(j, k):
+        target = lax.rem(y + k, ny)
+        cols = pl.ds(j * step, step)
+        return push(send_ref.at[target, :, cols], came.at[y, :, cols], y_send.at[j, k - 1],
+                    y_recv.at[j, k - 1], {"y": target})
+
+    def x_copy(kind, j, h):
+        cols = pl.ds(j * step, step)
+        source = {RIGHT: mine, LEFT: mine, PAIR: mine,
+                  FAR: (x_left if h == 0 else x_right) * 2 + c,
+                  PAIR_L: x_left * 2 + c, PAIR_R: x_right * 2 + c, PAIR_FAR: x_far * 2 + c}[kind]
+        if kind == RIGHT or (kind == FAR and h == 0):
+            where = {"x": x_right}
+        elif kind == LEFT or kind == FAR:
+            where = {"x": x_left}
+        else:
+            where = {"c": 1 - c}
+        ref = outs[h].at[source, :, cols]
+        return push(ref, ref, x_send.at[kind, j, h], x_recv.at[kind, j, h], where)
+
+    def both(kind, j):
+        return [x_copy(kind, j, h) for h in range(2)]
+
+    started = []
+
+    def start(copies):
+        for copy in copies:
+            copy.start()
+        started.extend(copies)
+
+    def pass_near(j):
+        for kind, forward, h in ((RIGHT, PAIR_L, 0), (LEFT, PAIR_R, 1)):
+            for copy in both(kind, j):
+                copy.wait_recv()
+            start([x_copy(FAR, j, h)] + both(forward, j))
+
+    def pass_far(j):
+        for h in range(2):
+            x_copy(FAR, j, h).wait_recv()
+            start([x_copy(PAIR_FAR, j, h)])
+
+    def z_next(s):
+        for way in range(2):
+            z_copy(way, s - 1).wait_recv()
+            start([z_copy(way, s)])
+
+    start([z_copy(0, 0), z_copy(1, 0)])
+    for j in range(chunks):
+        start([y_copy(j, k) for k in range(1, ny)])
+    came[pl.ds(y, 1)] = send_ref[pl.ds(y, 1)]
+    wall_ref[pl.ds(z, 1)] = w_ref[...].reshape(1, *w_ref.shape)
+    z_steps = list(range(1, nz // 2))
+    for j in range(chunks):
+        cols = pl.ds(j * step, step)
+        for k in range(1, ny):
+            y_copy(j, k).wait_recv()
+        block = came[:, :, cols].reshape(came.shape[0] * came.shape[1], step)
+        packed = dot(squeeze_ref[...], block).astype(BF)
+        tok_ref[pl.ds(mine, 1), :, cols] = packed[:rows].reshape(1, rows, step)
+        scl_ref[pl.ds(mine, 1), :, cols] = packed[rows:].reshape(1, rows, step)
+        start(both(RIGHT, j) + both(LEFT, j) + both(PAIR, j))
+        if j >= 1:
+            pass_near(j - 1)
+            if z_steps:
+                z_next(z_steps.pop(0))
+        if j >= 2:
+            pass_far(j - 2)
+    pass_near(chunks - 1)
+    for s in z_steps:
+        z_next(s)
+    for j in range(max(chunks - 2, 0), chunks):
+        pass_far(j)
+    for way in range(2):
+        z_copy(way, nz // 2 - 1).wait_recv()
+    for j in range(chunks):
+        for kind in (PAIR, PAIR_L, PAIR_R, PAIR_FAR):
+            for copy in both(kind, j):
+                copy.wait_recv()
+    for copy in started:
+        copy.wait_send()
+
+
+def gather(send, weights):
+    nz, ny, nx = lax.axis_size("dp"), lax.axis_size("y"), lax.axis_size("x")
+    width = send.shape[2]
+    chunks = 4
+    rows = ny * CAP
+    vmem = pl.BlockSpec(memory_space=pltpu.VMEM)
+    block = jax.ShapeDtypeStruct((2 * nx, rows, width), BF)
+    return pl.pallas_call(
+        functools.partial(gather_kernel, nz, ny, nx, chunks),
+        out_shape=(block, block, jax.ShapeDtypeStruct((nz, *weights.shape), BF)),
+        in_specs=[vmem] * 3,
+        out_specs=(vmem,) * 3,
+        scratch_shapes=[
+            pltpu.VMEM(send.shape, BF),
+            pltpu.SemaphoreType.DMA((chunks, ny - 1)),
+            pltpu.SemaphoreType.DMA((chunks, ny - 1)),
+            pltpu.SemaphoreType.DMA((7, chunks, 2)),
+            pltpu.SemaphoreType.DMA((7, chunks, 2)),
+            pltpu.SemaphoreType.DMA((2, nz // 2)),
+            pltpu.SemaphoreType.DMA((2, nz // 2)),
+        ],
+        compiler_params=pltpu.CompilerParams(
+            collective_id=0, has_side_effects=True, vmem_limit_bytes=32 << 20
+        ),
+        name="gather_rows",
+    )(send, weights, squeeze_matrix(ny))
 
 
 def routing(route_ids, route_gates, groups):
@@ -46,23 +205,15 @@
     send = jnp.concatenate(
         [token_slots.reshape(groups, PAD, width), scaled_slots.reshape(groups, PAD, width)], axis=1
     )
-    w_all = lax.all_gather(
-        jnp.concatenate([gate_w, up_w, down_w], axis=1), "dp", axis=0, tiled=True
-    )
+    rows = groups * CAP
+    token_rows, scaled_rows, w_all = gather(
+        send, jnp.concatenate([gate_w, up_w, down_w], axis=1)
+    )
+    n_slices = token_rows.shape[0]
+    token_rows = token_rows.reshape(n_slices * rows, width)
+    scaled_rows = scaled_rows.reshape(n_slices * rows, width)
+    w_all = w_all.reshape(width, 3 * hid)
     w_gate, w_up, w_down = w_all[:, :hid], w_all[:, hid : 2 * hid], w_all[:, 2 * hid :]
-    came = lax.all_to_all(send, "y", split_axis=0, concat_axis=0, tiled=True)
-    rows = groups * CAP
-    out_row = lax.broadcasted_iota(jnp.int32, (2 * rows, groups * 2 * PAD), 0)
-    in_row = lax.broadcasted_iota(jnp.int32, (2 * rows, groups * 2 * PAD), 1)
-    kind = (out_row >= rows).astype(jnp.int32)
-    local = out_row - kind * rows
-    wanted = (local // CAP) * (2 * PAD) + kind * PAD + local % CAP
-    squeeze = (in_row == wanted).astype(BF)
-    compact = dot(squeeze, came.reshape(groups * 2 * PAD, width)).astype(BF)
-    both = lax.all_gather(compact, ("x", "c"), axis=0, tiled=False)
-    n_slices = both.shape[0]
-    token_rows = both[:, :rows].reshape(n_slices * rows, width)
-    scaled_rows = both[:, rows:].reshape(n_slices * rows, width)
 
     gate_pre = dot(token_rows, w_gate)
     up_pre = dot(token_rows, w_up)
@@ -89,7 +240,7 @@
         axis=1,
     ).astype(BF)
     grads = lax.psum_scatter(grads, "dp", scatter_dimension=0, tiled=True)
-    back = dot(squeeze, summed, CONTRACT_ROWS).astype(BF).reshape(groups, 2 * PAD, width)
+    back = dot(squeeze_matrix(groups), summed, CONTRACT_ROWS).astype(BF).reshape(groups, 2 * PAD, width)
     back = lax.all_to_all(back, "y", split_axis=0, concat_axis=0, tiled=True)
     back = back.reshape(groups * 2 * PAD, width)
 

time: 256 us -> 178 us (0.70)
  waiting for transfers between devices: 183 us -> 71 us
  Pallas kernels: 0 us -> 52.9 us
  starting transfers between devices: 14.2 us -> 6.38 us
  matrix products: 22.1 us -> 17.2 us
  local copies, waits for them, and re-layouts: 12 us -> 7.19 us
    all_gather x2 -> x0, waiting for transfers between devices: 84.7 us -> none  [the longest x1 44 us: shards(): both = lax.all_gather(compact, ('x', 'c'), axis=0, tiled=False)]
    pallas_call x0 -> x1, Pallas kernels: none -> 52.9 us  [gather(): pl.pallas_call(functools.partial(gather_kernel, nz, ny, nx, chunks), out_...]
    all_to_all x1 -> x0, waiting for transfers between devices: 24.1 us -> none  [shards(): came = lax.all_to_all(send, 'y', split_axis=0, concat_axis=0, tiled=True)]
    all_to_all x1 -> x0, starting transfers between devices: 7.64 us -> none  [shards(): came = lax.all_to_all(send, 'y', split_axis=0, concat_axis=0, tiled=True)]
    slice x1 -> x0, local copies, waits for them, and re-layouts: 5.48 us -> none  [shards(): scaled_rows = both[:, rows:].reshape(n_slices * rows, width)]
    dot_general x18 -> x17, matrix products: 22.1 us -> 17.2 us  [dot(): return lax.dot_general(a, b, dims, preferred_element_type=F32)]
    reduce_scatter x1, waiting for transfers between devices: 33.8 us -> 30.8 us  [shards(): lax.psum_scatter(parts, ('x', 'c'), scatter_dimension=0, tiled=True)]
    unnamed x5 -> x3, waiting for transfers between devices: 40.4 us -> 40.2 us
  transfers between devices with their start and end apart: 6 -> 3, of which waited for: 5 -> 2; matrix products, arithmetic and copies ran while one was open for 8% -> 8% of each run, Pallas kernels for 0% -> 0%
where the time goes in v2:
time: 178 us; the launch traced here: 175 us
  waiting for transfers between devices  71 us (40%)
  Pallas kernels  52.9 us (30%)
  matrix products  17.2 us (10%)
  between operations  14.3 us (8%)
  local copies, waits for them, and re-layouts  7.19 us (4%)
  starting transfers between devices  6.38 us (4%)
  other arithmetic  6.18 us (3%)
    pallas_call x1, Pallas kernels, gather(): pl.pallas_call(functools.partial(gather_kernel, nz, ny, nx, chunks), out_...  52.9 us
    unnamed x3, waiting for transfers between devices  40.2 us
    reduce_scatter x1, waiting for transfers between devices, shards(): lax.psum_scatter(parts, ('x', 'c'), scatter_dimension=0, tiled=True)  30.8 us
    dot_general x17, matrix products, dot(): return lax.dot_general(a, b, dims, preferred_element_type=F32)  17.2 us
    all_to_all x1, starting transfers between devices, shards(): back = lax.all_to_all(back, 'y', split_axis=0, concat_axis=0, tiled=True)  6.3 us
    unnamed x19, local copies, waits for them, and re-layouts  5.28 us
  transfers between devices with their start and end apart: 3, of which 2 were waited for; matrix products, arithmetic and copies ran while one was open for 8% of the time, Pallas kernels for 0%

profile of v2, /device:TPU:1, one launch (start us, length us, event | category | flops | bytes accessed | tf_op | source)
XLA Modules:
  0.0 175.2 jit_solution(966560027368366062)
XLA Ops:
  7.3 0.8 convert_reduce_fusion
  8.5 1.5 fusion.6
  10.5 52.9 %gather_rows.1 = (bf16[8,48,3584]{2,1,0:T(8,128)(2,1)S(1)}, bf16[8,48,3584]{2,1,0:T(8,128)(2,1)S(1)}, bf16[8,448,384]{2,1,0:T(8,128)(2,1)S(1)}) custom-call(bf16[8,16,3584]{2,1,0:T(8,128)(2,1)S(1)} %pad_maximum_fusion.2.send_ref, bf16[448,384]{1,0:T(8,128)(2,1)S(1)} %pad_maximum_fusion.3.w_ref, bf16[96,128]{1,0:T(8,128)(2,1)S(1)} %copy-done.4), custom_call_target="tpu_custom_call" | custom-call | tf_op jit(solution)/shard_map/gather_rows/pallas_call | solution.py:157
  63.4 0.9 fusion.15
  64.3 0.9 fusion.7
  65.2 0.7 copy-done.3
  65.9 0.9 multiply_convert_fusion.2
  66.8 0.9 convolution_convert_fusion
  67.6 0.9 fusion.13
  68.5 0.9 fusion
  69.4 2.7 %pad_maximum_fusion = bf16[8,96,3584]{2,1,0:T(8,128)(2,1)} fusion(bf16[8,48,3584]{2,1,0:T(8,128)(2,1)S(1)} %bitcast.76, bf16[8,48,3584]{2,1,0:T(8,128)(2,1)S(1)} %bitcast.75), kind=kLoop, calls=%fused_computation.3 | loop fusion | flops 11010048 | bytes 11010048 | tf_op jit(solution)/shard_map/concatenate | solution.py:230
  72.2 2.6 %convolution_convert_fusion.1 = bf16[3584,128]{0,1:T(8,128)(2,1)S(1)} fusion(bf16[384,3584]{1,0:T(8,128)(2,1)} %bitcast.66, bf16[384,128]{1,0:T(8,128)(2,1)S(1)} %get-tuple-element.32), kind=kOutput, calls=%fused_computation.10 | convolution fusion | flops 352780288 | bytes 3768320 | tf_op jit(solution)/shard_map/dot_general | solution.py:21
  74.9 0.7 convolution_convert_fusion.2
  75.6 0.7 convolution_convert_fusion.3
  76.3 1.8 %pad_maximum_fusion.1 = bf16[3584,384]{0,1:T(8,128)(2,1)} fusion(bf16[3584,128]{0,1:T(8,128)(2,1)S(1)} %convolution_convert_fusion.1, bf16[3584,128]{0,1:T(8,128)(2,1)S(1)} %convolution_convert_fusion.2, bf16[3584,128]{0,1:T(8,128)(2,1)S(1)} %convolution_convert_fusion.3), kind=kLoop, calls=%fused_computation.19 | loop fusion | flops 8257536 | bytes 5505024 | tf_op jit(solution)/shard_map/concatenate | solution.py:234
  78.1 4.6 %copy.29 = bf16[3584,384]{1,0:T(8,128)(2,1)} copy(bf16[3584,384]{0,1:T(8,128)(2,1)} %pad_maximum_fusion.1) | data formatting | bytes 5505024
  82.7 30.8 %reduce-scatter.5.cloned.1.call-done = bf16[96,3584]{1,0:T(8,128)(2,1)} async-done(((bf16[768,3584]{1,0:T(8,128)(2,1)}), bf16[96,3584]{1,0:T(8,128)(2,1)}) %reduce-scatter.5.cloned.1.call-update) | async-done | bytes 688144 | tf_op jit(solution)/shard_map/reduce_scatter | solution.py:233
  113.5 2.5 %convolution_convert_fusion.4 = bf16[3584,128]{0,1:T(8,128)(2,1)} fusion(bf16[96,3584]{1,0:T(8,128)(2,1)} %reduce-scatter.5.cloned.1.call-done, bf16[96,128]{1,0:T(8,128)(2,1)S(1)} %copy-done.4), kind=kOutput, calls=%fused_computation.13 | convolution fusion | flops 88539136 | bytes 1630208 | tf_op jit(solution)/shard_map/dot_general | solution.py:21
  115.9 6.3 %all-to-all-start = ((bf16[8,16,3584]{2,1,0:T(8,128)(2,1)}), bf16[8,16,3584]{2,1,0:T(8,128)(2,1)S(1)}, u32[]{:S(2)}, u32[]{:S(2)}) async-start(bf16[8,16,3584]{2,1,0:T(8,128)(2,1)} %bitcast.12), calls=%async_computation.1 | async-start | bytes 1835008 | tf_op jit(solution)/shard_map/all_to_all | solution.py:244
  122.3 40.2 %reduce-scatter.7.cloned.1.call-done = bf16[448,384]{1,0:T(8,128)(2,1)} async-done(((bf16[3584,384]{1,0:T(8,128)(2,1)}), bf16[448,384]{1,0:T(8,128)(2,1)}) %reduce-scatter.7.cloned.1.call-update) | async-done | bytes 344080
  162.4 1.7 fusion.33
  164.6 0.6 select_reduce_fusion
  165.6 1.3 fusion.2
  167.0 1.3 fusion.3
  (34 shorter events, 1.8 us)
Async XLA Ops:
  7.2 2.8 %copy-start = (bf16[128,3584]{1,0:T(8,128)(2,1)S(1)}, bf16[128,3584]{1,0:T(8,128)(2,1)}, u32[]{:S(2)}) copy-start(bf16[128,3584]{1,0:T(8,128)(2,1)} %param.10) | copy-start | bytes 2752516
  7.2 3.3 %copy-start.4 = (bf16[96,128]{1,0:T(8,128)(2,1)S(1)}, bf16[96,128]{1,0:T(8,128)(2,1)}, u32[]{:S(2)}) copy-start(bf16[96,128]{1,0:T(8,128)(2,1)} %constant.14.clone.squeeze_ref) | copy-start | bytes 73732
  7.2 3.2 %copy-start.7 = (bf16[448,128]{1,0:T(8,128)(2,1)S(1)}, bf16[448,128]{1,0:T(8,128)(2,1)}, u32[]{:S(2)}) copy-start(bf16[448,128]{1,0:T(8,128)(2,1)} %param.13) | copy-start | bytes 344068
  7.2 3.2 %copy-start.6 = (bf16[448,128]{1,0:T(8,128)(2,1)S(1)}, bf16[448,128]{1,0:T(8,128)(2,1)}, u32[]{:S(2)}) copy-start(bf16[448,128]{1,0:T(8,128)(2,1)} %param.14) | copy-start | bytes 344068
  7.2 3.2 %copy-start.5 = (bf16[448,128]{1,0:T(8,128)(2,1)S(1)}, bf16[448,128]{1,0:T(8,128)(2,1)}, u32[]{:S(2)}) copy-start(bf16[448,128]{1,0:T(8,128)(2,1)} %param.15) | copy-start | bytes 344068
  7.2 106.2 %reduce-scatter.5.cloned.1.call-start = ((), (), s32[]{:S(2)}) async-start(), calls=%async_computation.3 | async-start | bytes 6193152 | tf_op jit(solution)/shard_map/reduce_scatter | solution.py:233
  63.4 1.8 %copy-start.1 = (bf16[8,48,3584]{2,1,0:T(8,128)(2,1)}, bf16[8,48,3584]{2,1,0:T(8,128)(2,1)S(1)}, u32[]{:S(2)}) copy-start(bf16[8,48,3584]{2,1,0:T(8,128)(2,1)S(1)} %get-tuple-element.9) | copy-start | bytes 8257540
  63.4 2.4 %copy-start.3 = (bf16[8,48,3584]{2,1,0:T(8,128)(2,1)}, bf16[8,48,3584]{2,1,0:T(8,128)(2,1)S(1)}, u32[]{:S(2)}) copy-start(bf16[8,48,3584]{2,1,0:T(8,128)(2,1)S(1)} %get-tuple-element.11) | copy-start | bytes 8257540
  72.2 90.2 %reduce-scatter.7.cloned.1.call-start = ((), (), s32[]{:S(2)}) async-start(), calls=%async_computation.4 | async-start | bytes 3096576
  72.2 2.6 %copy-start.2 = (bf16[8,48,3584]{2,1,0:T(8,128)(2,1)S(1)}, bf16[8,48,3584]{2,1,0:T(8,128)(2,1)}, u32[]{:S(2)}) copy-start(bf16[8,48,3584]{2,1,0:T(8,128)(2,1)} %copy-done.1) | copy-start | bytes 8257540
  82.7 81.9 %copy-start.8 = (s32[128,8]{0,1:T(8,128)S(1)}, s32[128,8]{0,1:T(8,128)}, u32[]{:S(2)}) copy-start(s32[128,8]{0,1:T(8,128)} %param.11) | copy-start | bytes 12292
  115.9 48.2 %all-to-all-start = ((bf16[8,16,3584]{2,1,0:T(8,128)(2,1)}), bf16[8,16,3584]{2,1,0:T(8,128)(2,1)S(1)}, u32[]{:S(2)}, u32[]{:S(2)}) async-start(bf16[8,16,3584]{2,1,0:T(8,128)(2,1)} %bitcast.12), calls=%async_computation.1 | async-start | bytes 1835008 | tf_op jit(solution)/shard_map/all_to_all | solution.py:244
Sparse Core Ops, SparseCore 0:
  72.3 41.1 reduce-scatter.4
  116.3 46.0 reduce-scatter.6

commit v3 on v2

--- a/solution.py
+++ b/solution.py
@@ -175,6 +175,189 @@
     )(send, weights, squeeze_matrix(ny))
 
 
+def scatter_kernel(nz, ny, nx, chunks, out_ref, dx_ref, g_ref, expand_ref,
+                   back_ref, dg_ref, du_ref, dd_ref,
+                   pair, far_out, far_in, near_out, near_in, y_out, z_out, z_in,
+                   pair_send, pair_recv, far_send, far_recv, near_send, near_recv,
+                   y_send, y_recv, z_send, z_recv):
+    z, y, x, c = (lax.axis_index(n) for n in ("dp", "y", "x", "c"))
+    width = out_ref.shape[3]
+    rows = out_ref.shape[2]
+    step = width // chunks
+    block = g_ref.shape[1]
+    half = block // 2
+    last = nz // 2 - 1
+    x_right, x_left, x_far = (lax.rem(x + k, nx) for k in (1, nx - 1, 2))
+    z_right, z_left = lax.rem(z + 1, nz), lax.rem(z + nz - 1, nz)
+    parts = (out_ref, dx_ref)
+    peers = [{"y": lax.rem(y + k, ny)} for k in range(1, ny)]
+    peers += [{"x": x_right}, {"x": x_left}, {"c": 1 - c}, {"dp": z_right}, {"dp": z_left}]
+    barrier = pltpu.get_barrier_semaphore()
+    for peer in peers:
+        pl.semaphore_signal(barrier, inc=1, device_id=peer, device_id_type=pl.DeviceIdType.MESH)
+    pl.semaphore_wait(barrier, len(peers))
+    sides = ({"x": x_right}, {"x": x_left})
+    near = (x_right, x_left)
+
+    def pair_copy(j, h):
+        cols = pl.ds(j * step, step)
+        return push(parts[h].at[:, 1 - c, :, cols], pair.at[h, :, :, cols], pair_send.at[j, h],
+                    pair_recv.at[j, h], {"c": 1 - c})
+
+    def far_copy(j, h):
+        cols = pl.ds(j * step, step)
+        return push(far_out.at[h, :, cols], far_in.at[h, :, cols], far_send.at[j, h],
+                    far_recv.at[j, h], sides[h])
+
+    def near_copy(j, side, h):
+        cols = pl.ds(j * step, step)
+        return push(near_out.at[side, h, :, cols], near_in.at[side, h, :, cols],
+                    near_send.at[j, side, h], near_recv.at[j, side, h], sides[side])
+
+    def y_copy(j, k):
+        target = lax.rem(y + k, ny)
+        cols = pl.ds(j * step, step)
+        return push(y_out.at[target, :, cols], back_ref.at[y, :, cols], y_send.at[j, k - 1],
+                    y_recv.at[j, k - 1], {"y": target})
+
+    def z_part(way, s):
+        return pl.ds(way * half, half) if s == 0 else pl.ds(0, block)
+
+    def z_dest(way, s):
+        return lax.rem(z + (nz // 2 - s if way == 0 else nz // 2 + s), nz)
+
+    def z_copy(way, s):
+        part = z_part(way, s)
+        src = g_ref.at[z_dest(way, s), part, :] if s == 0 else z_out.at[way, s - 1]
+        return push(src, z_in.at[way, s, part, :], z_send.at[way, s], z_recv.at[way, s],
+                    {"dp": z_right if way == 0 else z_left})
+
+    started = []
+
+    def start(copy):
+        copy.start()
+        started.append(copy)
+
+    def z_next(s):
+        for way in range(2):
+            z_copy(way, s - 1).wait_recv()
+            dest = z_dest(way, s)
+            for k in range(2):
+                rows_k = pl.ds(k * half, half)
+                value = g_ref[dest, rows_k, :]
+                if s > 1 or k == way:
+                    value = (value.astype(F32) + z_in[way, s - 1, rows_k, :].astype(F32)).astype(BF)
+                z_out[way, s - 1, rows_k, :] = value
+            start(z_copy(way, s))
+
+    def chip_sum(j, h, owner):
+        cols = pl.ds(j * step, step)
+        return parts[h][owner, c, :, cols].astype(F32) + pair[h, owner, :, cols].astype(F32)
+
+    def first(j):
+        cols = pl.ds(j * step, step)
+        for h in range(2):
+            pair_copy(j, h).wait_recv()
+        for h in range(2):
+            far_out[h, :, cols] = chip_sum(j, h, x_far).astype(BF)
+            start(far_copy(j, h))
+        for side in range(2):
+            near_out[side, 1 - side, :, cols] = chip_sum(j, 1 - side, near[side]).astype(BF)
+            start(near_copy(j, side, 1 - side))
+
+    def middle(j):
+        cols = pl.ds(j * step, step)
+        for h in range(2):
+            far_copy(j, h).wait_recv()
+            value = chip_sum(j, h, near[h]) + far_in[h, :, cols].astype(F32)
+            near_out[h, h, :, cols] = value.astype(BF)
+            start(near_copy(j, h, h))
+
+    def finish(j):
+        cols = pl.ds(j * step, step)
+        sums = []
+        for h in range(2):
+            value = chip_sum(j, h, x)
+            for side in range(2):
+                near_copy(j, side, h).wait_recv()
+                value = value + near_in[side, h, :, cols].astype(F32)
+            sums.append(value.astype(BF))
+        value = dot(expand_ref[...], jnp.concatenate(sums, axis=0)).astype(BF)
+        y_out[:, :, cols] = value.reshape(ny, value.shape[0] // ny, step)
+        for k in range(1, ny):
+            start(y_copy(j, k))
+        back_ref[pl.ds(y, 1), :, cols] = y_out[pl.ds(y, 1), :, cols]
+
+    for j in range(chunks):
+        for h in range(2):
+            start(pair_copy(j, h))
+    for way in range(2):
+        start(z_copy(way, 0))
+    z_steps = list(range(1, last + 1))
+    for j in range(chunks):
+        first(j)
+        if j >= 1:
+            middle(j - 1)
+        if j >= 2:
+            finish(j - 2)
+        if j >= 1 and z_steps:
+            z_next(z_steps.pop(0))
+    middle(chunks - 1)
+    for j in range(max(chunks - 2, 0), chunks):
+        finish(j)
+    for s in z_steps:
+        z_next(s)
+    for way in range(2):
+        z_copy(way, last).wait_recv()
+    hid = dg_ref.shape[1]
+    for k, ref in enumerate((dg_ref, du_ref, dd_ref)):
+        cols = pl.ds(k * hid, hid)
+        total = g_ref[z, :, cols].astype(F32)
+        for way in range(2):
+            total = total + z_in[way, last, :, cols].astype(F32)
+        ref[...] = total.astype(BF)
+    for j in range(chunks):
+        for k in range(1, ny):
+            y_copy(j, k).wait_recv()
+    for copy in started:
+        copy.wait_send()
+
+
+def scatter(out_part, dx_part, grads):
+    nz, ny, nx = lax.axis_size("dp"), lax.axis_size("y"), lax.axis_size("x")
+    rows, width = out_part.shape[2:]
+    block, cols = grads.shape[1:]
+    chunks = 4
+    vmem = pl.BlockSpec(memory_space=pltpu.VMEM)
+    sems = pltpu.SemaphoreType.DMA
+    grad = jax.ShapeDtypeStruct((block, cols // 3), BF)
+    return pl.pallas_call(
+        functools.partial(scatter_kernel, nz, ny, nx, chunks),
+        out_shape=(jax.ShapeDtypeStruct((ny, 2 * PAD, width), BF), grad, grad, grad),
+        in_specs=[vmem] * 4,
+        out_specs=(vmem,) * 4,
+        scratch_shapes=[
+            pltpu.VMEM((2, nx, rows, width), BF),
+            pltpu.VMEM((2, rows, width), BF),
+            pltpu.VMEM((2, rows, width), BF),
+            pltpu.VMEM((2, 2, rows, width), BF),
+            pltpu.VMEM((2, 2, rows, width), BF),
+            pltpu.VMEM((ny, 2 * PAD, width), BF),
+            pltpu.VMEM((2, nz // 2 - 1, block, cols), BF),
+            pltpu.VMEM((2, nz // 2, block, cols), BF),
+            sems((chunks, 2)), sems((chunks, 2)),
+            sems((chunks, 2)), sems((chunks, 2)),
+            sems((chunks, 2, 2)), sems((chunks, 2, 2)),
+            sems((chunks, ny - 1)), sems((chunks, ny - 1)),
+            sems((2, nz // 2)), sems((2, nz // 2)),
+        ],
+        compiler_params=pltpu.CompilerParams(
+            collective_id=1, has_side_effects=True, vmem_limit_bytes=48 << 20
+        ),
+        name="scatter_sums",
+    )(out_part, dx_part, grads, squeeze_matrix(ny).T)
+
+
 def routing(route_ids, route_gates, groups):
     tok_rows = route_ids.shape[0]
     experts = jnp.arange(groups, dtype=jnp.int32)
@@ -227,10 +410,6 @@
     dx_part = (
         dot(d_gate_pre, w_gate, CONTRACT_COLS) + dot(d_up_pre, w_up, CONTRACT_COLS)
     ).astype(BF)
-    parts = jnp.concatenate(
-        [out_part.reshape(n_slices, rows, width), dx_part.reshape(n_slices, rows, width)], axis=1
-    ).reshape(n_slices * 2 * rows, width)
-    summed = lax.psum_scatter(parts, ("x", "c"), scatter_dimension=0, tiled=True)
     grads = jnp.concatenate(
         [
             dot(token_rows, d_gate_pre, CONTRACT_ROWS),
@@ -239,9 +418,11 @@
         ],
         axis=1,
     ).astype(BF)
-    grads = lax.psum_scatter(grads, "dp", scatter_dimension=0, tiled=True)
-    back = dot(squeeze_matrix(groups), summed, CONTRACT_ROWS).astype(BF).reshape(groups, 2 * PAD, width)
-    back = lax.all_to_all(back, "y", split_axis=0, concat_axis=0, tiled=True)
+    back, d_gate_w, d_up_w, d_down_w = scatter(
+        out_part.reshape(n_slices // 2, 2, rows, width),
+        dx_part.reshape(n_slices // 2, 2, rows, width),
+        grads.reshape(width // gate_w.shape[0], gate_w.shape[0], 3 * hid),
+    )
     back = back.reshape(groups * 2 * PAD, width)
 
     zero = jnp.zeros_like(sel)
@@ -255,14 +436,7 @@
     inner = dot(back, cotangent, CONTRACT_COLS) * member_out
     by_expert = jnp.sum(inner.reshape(groups, 2 * PAD, tok_rows), axis=1).T
     d_gates = jnp.sum(jnp.where(match, by_expert[:, None, :], 0.0), axis=2)
-    return (
-        moe_out,
-        d_tokens,
-        d_gates,
-        grads[:, :hid],
-        grads[:, hid : 2 * hid],
-        grads[:, 2 * hid :],
-    )
+    return moe_out, d_tokens, d_gates, d_gate_w, d_up_w, d_down_w
 
 
 def solution(mesh):

time: 178 us -> 138 us (0.78); the launches traced: 175 us -> 137 us
  waiting for transfers between devices: 71 us -> 0 us
  Pallas kernels: 52.9 us -> 100 us
  between operations: 14.3 us -> 0.9 us
  local copies, waits for them, and re-layouts: 7.19 us -> 13.8 us
  starting transfers between devices: 6.38 us -> 0 us
  other arithmetic: 6.18 us -> 3.57 us
    pallas_call x0 -> x1, Pallas kernels: none -> 47.3 us  [scatter(): pl.pallas_call(functools.partial(scatter_kernel, nz, ny, nx, chunks), out...]
    unnamed x3 -> x0, waiting for transfers between devices: 40.2 us -> none
    reduce_scatter x1 -> x0, waiting for transfers between devices: 30.8 us -> none  [shards(): lax.psum_scatter(parts, ('x', 'c'), scatter_dimension=0, tiled=True)]
    dot_general x0 -> x2, local copies, waits for them, and re-layouts: none -> 9.28 us  [dot(): return lax.dot_general(a, b, dims, preferred_element_type=F32)]
    all_to_all x1 -> x0, starting transfers between devices: 6.3 us -> none  [shards(): back = lax.all_to_all(back, 'y', split_axis=0, concat_axis=0, tiled=True)]
    concatenate x1 -> x0, other arithmetic: 2.74 us -> none  [shards(): jnp.concatenate([out_part.reshape(n_slices, rows, width), dx_part.reshape...]
    dot_general x17 -> x16, matrix products: 17.2 us -> 18.6 us  [dot(): return lax.dot_general(a, b, dims, preferred_element_type=F32)]
    unnamed x19 -> x27, local copies, waits for them, and re-layouts: 5.28 us -> 4.3 us
  transfers between devices with their start and end apart: 3 -> 0, of which waited for: 2 -> 0; matrix products, arithmetic and copies ran while one was open for 8% -> 0% of each run, Pallas kernels for 0% -> 0%
where the time goes in v3:
time: 138 us; the launch traced here: 137 us
  Pallas kernels  100 us (72%)
  matrix products  18.6 us (13%)
  local copies, waits for them, and re-layouts  13.8 us (10%)
  other arithmetic  3.57 us (3%)
    pallas_call x1, Pallas kernels, gather(): pl.pallas_call(functools.partial(gather_kernel, nz, ny, nx, chunks), out_...  53 us
    pallas_call x1, Pallas kernels, scatter(): pl.pallas_call(functools.partial(scatter_kernel, nz, ny, nx, chunks), out...  47.3 us
    dot_general x16, matrix products, dot(): return lax.dot_general(a, b, dims, preferred_element_type=F32)  18.6 us
    dot_general x2, local copies, waits for them, and re-layouts, dot(): return lax.dot_general(a, b, dims, preferred_element_type=F32)  9.28 us
    unnamed x27, local copies, waits for them, and re-layouts  4.3 us

profile of v3, /device:TPU:1, one launch (start us, length us, event | category | flops | bytes accessed | tf_op | source)
XLA Modules:
  0.0 137.2 jit_solution(15222803371451916942)
XLA Ops:
  0.7 0.8 convert_reduce_fusion
  2.3 1.5 %fusion.6 = bf16[8,8,3584]{2,1,0:T(8,128)(2,1)S(1)} fusion(bf16[128,3584]{1,0:T(8,128)(2,1)} %param.9, f32[64]{0:T(128)S(1)} %eq.45, f32[8,128]{1,0:T(8,128)S(1)} %convolution_select_fusion), kind=kOutput, calls=%fused_computation.13 | convolution fusion | flops 58974208 | bytes 1380608 | tf_op jit(solution)/shard_map/dot_general | solution.py:21
  4.0 53.0 %gather_rows.1 = (bf16[8,48,3584]{2,1,0:T(8,128)(2,1)S(1)}, bf16[8,48,3584]{2,1,0:T(8,128)(2,1)S(1)}, bf16[8,448,384]{2,1,0:T(8,128)(2,1)S(1)}) custom-call(bf16[8,16,3584]{2,1,0:T(8,128)(2,1)S(1)} %pad_maximum_fusion.1.send_ref, bf16[448,384]{1,0:T(8,128)(2,1)S(1)} %pad_maximum_fusion.2.w_ref, bf16[96,128]{1,0:T(8,128)(2,1)S(1)} %copy-done.6), custom_call_target="tpu_custom_call" | custom-call | tf_op jit(solution)/shard_map/gather_rows/pallas_call | solution.py:157
  57.1 0.9 fusion.11
  57.9 0.9 fusion.15
  59.4 0.8 copy-done.4
  60.2 0.9 multiply_convert_fusion
  61.1 4.8 %copy.25 = bf16[3584,384]{1,0:T(8,128)(2,1)} copy(bf16[3584,384]{0,1:T(8,128)(2,1)} %bitcast.78) | data formatting | bytes 5505024 | tf_op jit(solution)/shard_map/dot_general | solution.py:21
  65.8 2.7 %convolution_convert_fusion.2 = bf16[8,448,128]{2,1,0:T(8,128)(2,1)S(1)} fusion(bf16[8,448,384]{2,1,0:T(8,128)(2,1)} %bitcast.82, bf16[384,128]{1,0:T(8,128)(2,1)S(1)} %get-tuple-element.24), kind=kOutput, calls=%fused_computation.15 | convolution fusion | flops 352780288 | bytes 3768320 | tf_op jit(solution)/shard_map/dot_general | solution.py:21
  68.5 4.5 %copy.24 = bf16[3584,384]{1,0:T(8,128)(2,1)} copy(bf16[3584,384]{0,1:T(8,128)(2,1)} %bitcast.76) | data formatting | bytes 5505024 | tf_op jit(solution)/shard_map/dot_general | solution.py:21
  73.0 2.8 %convolution_convert_fusion.3 = bf16[8,448,128]{2,1,0:T(8,128)(2,1)S(1)} fusion(bf16[8,448,384]{2,1,0:T(8,128)(2,1)} %bitcast.79, bf16[384,128]{1,0:T(8,128)(2,1)S(1)} %get-tuple-element.22), kind=kOutput, calls=%fused_computation.16 | convolution fusion | flops 352780288 | bytes 3768320 | tf_op jit(solution)/shard_map/dot_general | solution.py:21
  75.8 0.9 convolution_convert_fusion.4
  76.7 1.9 %pad_maximum_fusion.g_ref = bf16[8,448,384]{2,1,0:T(8,128)(2,1)} fusion(bf16[8,448,128]{2,1,0:T(8,128)(2,1)S(1)} %convolution_convert_fusion.2, bf16[8,448,128]{2,1,0:T(8,128)(2,1)S(1)} %convolution_convert_fusion.3, bf16[8,448,128]{2,1,0:T(8,128)(2,1)S(1)} %convolution_convert_fusion.4), kind=kLoop, calls=%fused_computation.14 | loop fusion | flops 8257536 | bytes 5505024 | tf_op jit(solution)/shard_map/concatenate | solution.py:413
  78.7 0.8 copy-done.2
  79.5 0.9 fusion.13
  80.4 2.4 %fusion = bf16[384,3584]{1,0:T(8,128)(2,1)} fusion(f32[384,3584]{1,0:T(8,128)S(1)} %fusion.13, bf16[384,128]{1,0:T(8,128)(2,1)S(1)} %get-tuple-element.22, bf16[3584,384]{1,0:T(8,128)(2,1)S(1)} %bitcast.72), kind=kOutput, calls=%fused_computation.1 | convolution fusion | flops 355074048 | bytes 9273344 | tf_op jit(solution)/shard_map/dot_general | solution.py:21
  82.8 0.9 convolution_convert_fusion
  83.7 47.3 %scatter_sums.1 = (bf16[8,16,3584]{2,1,0:T(8,128)(2,1)S(1)}, bf16[448,128]{1,0:T(8,128)(2,1)S(1)}, bf16[448,128]{1,0:T(8,128)(2,1)S(1)}, bf16[448,128]{1,0:T(8,128)(2,1)S(1)}) custom-call(bf16[4,2,48,3584]{3,2,1,0:T(8,128)(2,1)S(1)} %bitcast.67, bf16[4,2,48,3584]{3,2,1,0:T(8,128)(2,1)} %bitcast.81, bf16[8,448,384]{2,1,0:T(8,128)(2,1)} %pad_maximum_fusion.g_ref, ...), custom_call_target="tpu_custom_call" | custom-call | tf_op jit(solution)/shard_map/scatter_sums/pallas_call | solution.py:334
  131.5 1.3 fusion.2
  132.9 1.3 fusion.3
  134.6 0.6 select_reduce_fusion
  135.2 0.6 copy.29
  135.9 0.6 copy.30
  136.5 0.6 copy.31
  (34 shorter events, 2.4 us)
Async XLA Ops:
  0.6 1.4 %copy-start = (bf16[128,3584]{1,0:T(8,128)(2,1)S(1)}, bf16[128,3584]{1,0:T(8,128)(2,1)}, u32[]{:S(2)}) copy-start(bf16[128,3584]{1,0:T(8,128)(2,1)} %param.10) | copy-start | bytes 2752516
  0.6 3.4 %copy-start.6 = (bf16[96,128]{1,0:T(8,128)(2,1)S(1)}, bf16[96,128]{1,0:T(8,128)(2,1)}, u32[]{:S(2)}) copy-start(bf16[96,128]{1,0:T(8,128)(2,1)} %constant.14.clone.squeeze_ref) | copy-start | bytes 73732
  0.7 3.3 %copy-start.10 = (bf16[448,128]{1,0:T(8,128)(2,1)S(1)}, bf16[448,128]{1,0:T(8,128)(2,1)}, u32[]{:S(2)}) copy-start(bf16[448,128]{1,0:T(8,128)(2,1)} %param.13) | copy-start | bytes 344068
  0.7 3.3 %copy-start.9 = (bf16[448,128]{1,0:T(8,128)(2,1)S(1)}, bf16[448,128]{1,0:T(8,128)(2,1)}, u32[]{:S(2)}) copy-start(bf16[448,128]{1,0:T(8,128)(2,1)} %param.14) | copy-start | bytes 344068
  0.7 3.3 %copy-start.8 = (bf16[448,128]{1,0:T(8,128)(2,1)S(1)}, bf16[448,128]{1,0:T(8,128)(2,1)}, u32[]{:S(2)}) copy-start(bf16[448,128]{1,0:T(8,128)(2,1)} %param.15) | copy-start | bytes 344068
  57.0 1.8 %copy-start.3 = (bf16[8,48,3584]{2,1,0:T(8,128)(2,1)}, bf16[8,48,3584]{2,1,0:T(8,128)(2,1)S(1)}, u32[]{:S(2)}) copy-start(bf16[8,48,3584]{2,1,0:T(8,128)(2,1)S(1)} %get-tuple-element.13) | copy-start | bytes 8257540
  57.0 2.4 %copy-start.1 = (bf16[8,448,384]{2,1,0:T(8,128)(2,1)}, bf16[8,448,384]{2,1,0:T(8,128)(2,1)S(1)}, u32[]{:S(2)}) copy-start(bf16[8,448,384]{2,1,0:T(8,128)(2,1)S(1)} %get-tuple-element.14) | copy-start | bytes 8257540
  57.0 3.2 %copy-start.4 = (bf16[8,48,3584]{2,1,0:T(8,128)(2,1)}, bf16[8,48,3584]{2,1,0:T(8,128)(2,1)S(1)}, u32[]{:S(2)}) copy-start(bf16[8,48,3584]{2,1,0:T(8,128)(2,1)S(1)} %get-tuple-element.15) | copy-start | bytes 8257540
  73.0 2.8 %copy-start.7 = (bf16[3584,384]{1,0:T(8,128)(2,1)S(1)}, bf16[3584,384]{1,0:T(8,128)(2,1)}, u32[]{:S(2)}) copy-start(bf16[3584,384]{1,0:T(8,128)(2,1)} %copy.24) | copy-start | bytes 8257540
  76.7 2.8 %copy-start.2 = (bf16[8,448,384]{2,1,0:T(8,128)(2,1)S(1)}, bf16[8,448,384]{2,1,0:T(8,128)(2,1)}, u32[]{:S(2)}) copy-start(bf16[8,448,384]{2,1,0:T(8,128)(2,1)} %copy-done.1) | copy-start | bytes 8257540
  82.8 0.9 copy-start.5
  132.8 1.8 %copy-start.11 = (s32[128,8]{0,1:T(8,128)S(1)}, s32[128,8]{0,1:T(8,128)}, u32[]{:S(2)}) copy-start(s32[128,8]{0,1:T(8,128)} %param.11) | copy-start | bytes 12292

commit v4 on v3

--- a/solution.py
+++ b/solution.py
@@ -58,12 +58,12 @@
         pl.semaphore_signal(barrier, inc=1, device_id=peer, device_id_type=pl.DeviceIdType.MESH)
     pl.semaphore_wait(barrier, len(peers))
 
-    def z_copy(way, s):
+    def z_copy(way, s, q):
         source = lax.rem(z + (nz - s if way == 0 else s), nz)
-        part = pl.ds(0, 2 * half) if s < nz // 2 - 1 else pl.ds(way * half, half)
+        part = pl.ds(q * half, half)
         src = w_ref if s == 0 else wall_ref.at[source]
-        return push(src.at[part, :], wall_ref.at[source, part, :], z_send.at[way, s],
-                    z_recv.at[way, s], {"dp": z_right if way == 0 else z_left})
+        return push(src.at[part, :], wall_ref.at[source, part, :], z_send.at[way, s, q],
+                    z_recv.at[way, s, q], {"dp": z_right if way == 0 else z_left})
 
     def y_copy(j, k):
         target = lax.rem(y + k, ny)
@@ -106,17 +106,21 @@
             x_copy(FAR, j, h).wait_recv()
             start([x_copy(PAIR_FAR, j, h)])
 
-    def z_next(s):
+    last = nz // 2 - 1
+
+    def z_next(s, k):
         for way in range(2):
-            z_copy(way, s - 1).wait_recv()
-            start([z_copy(way, s)])
-
-    start([z_copy(0, 0), z_copy(1, 0)])
+            q = way if k == 0 else 1 - way
+            z_copy(way, s - 1, q).wait_recv()
+            if s < last or k == 0:
+                start([z_copy(way, s, q)])
+
+    start([z_copy(way, 0, way if k == 0 else 1 - way) for k in range(2) for way in range(2)])
     for j in range(chunks):
         start([y_copy(j, k) for k in range(1, ny)])
     came[pl.ds(y, 1)] = send_ref[pl.ds(y, 1)]
     wall_ref[pl.ds(z, 1)] = w_ref[...].reshape(1, *w_ref.shape)
-    z_steps = list(range(1, nz // 2))
+    z_steps = [(s, k) for s in range(1, nz // 2) for k in range(2)]
     for j in range(chunks):
         cols = pl.ds(j * step, step)
         for k in range(1, ny):
@@ -128,17 +132,17 @@
         start(both(RIGHT, j) + both(LEFT, j) + both(PAIR, j))
         if j >= 1:
             pass_near(j - 1)
-            if z_steps:
-                z_next(z_steps.pop(0))
         if j >= 2:
             pass_far(j - 2)
+        if j >= 2 and z_steps:
+            z_next(*z_steps.pop(0))
     pass_near(chunks - 1)
-    for s in z_steps:
-        z_next(s)
+    for s, k in z_steps:
+        z_next(s, k)
     for j in range(max(chunks - 2, 0), chunks):
         pass_far(j)
     for way in range(2):
-        z_copy(way, nz // 2 - 1).wait_recv()
+        z_copy(way, last, way).wait_recv()
     for j in range(chunks):
         for kind in (PAIR, PAIR_L, PAIR_R, PAIR_FAR):
             for copy in both(kind, j):
@@ -150,7 +154,7 @@
 def gather(send, weights):
     nz, ny, nx = lax.axis_size("dp"), lax.axis_size("y"), lax.axis_size("x")
     width = send.shape[2]
-    chunks = 4
+    chunks = 7
     rows = ny * CAP
     vmem = pl.BlockSpec(memory_space=pltpu.VMEM)
     block = jax.ShapeDtypeStruct((2 * nx, rows, width), BF)
@@ -165,14 +169,50 @@
             pltpu.SemaphoreType.DMA((chunks, ny - 1)),
             pltpu.SemaphoreType.DMA((7, chunks, 2)),
             pltpu.SemaphoreType.DMA((7, chunks, 2)),
-            pltpu.SemaphoreType.DMA((2, nz // 2)),
-            pltpu.SemaphoreType.DMA((2, nz // 2)),
+            pltpu.SemaphoreType.DMA((2, nz // 2, 2)),
+            pltpu.SemaphoreType.DMA((2, nz // 2, 2)),
         ],
         compiler_params=pltpu.CompilerParams(
-            collective_id=0, has_side_effects=True, vmem_limit_bytes=32 << 20
+            collective_id=0, has_side_effects=True, vmem_limit_bytes=18 << 20
         ),
         name="gather_rows",
     )(send, weights, squeeze_matrix(ny))
+
+
+def expert_kernel(tok_ref, scl_ref, w_ref, out_ref, dx_ref, g_ref):
+    width = tok_ref.shape[1]
+    hid = w_ref.shape[1] // 3
+    pre = dot(tok_ref[...], w_ref[:, : 2 * hid])
+    gate_pre, up_pre = pre[:, :hid], pre[:, hid:]
+    sig = jax.nn.sigmoid(gate_pre)
+    active = gate_pre * sig
+    hidden = (active * up_pre).astype(BF)
+    d_hidden = dot(scl_ref[...], w_ref[:, 2 * hid :])
+    d_gate_pre = (d_hidden * up_pre * sig * (1.0 + gate_pre * (1.0 - sig))).astype(BF)
+    d_up_pre = (d_hidden * active).astype(BF)
+    d_pre = jnp.concatenate([d_gate_pre, d_up_pre], axis=1)
+    d_pre_t, hidden_t = d_pre.T, hidden.T
+    pieces = 7
+    step = width // pieces
+    for n in range(pieces):
+        part = pl.ds(n * step, step)
+        g_ref[part, : 2 * hid] = dot(d_pre_t, tok_ref[:, part]).astype(BF).T
+        g_ref[part, 2 * hid :] = dot(hidden_t, scl_ref[:, part]).astype(BF).T
+        out_ref[:, part] = dot(hidden, w_ref[part, 2 * hid :], CONTRACT_COLS).astype(BF)
+        dx_ref[:, part] = dot(d_pre, w_ref[part, : 2 * hid], CONTRACT_COLS).astype(BF)
+
+
+def expert_math(token_rows, scaled_rows, w_all):
+    vmem = pl.BlockSpec(memory_space=pltpu.VMEM)
+    rows = jax.ShapeDtypeStruct(token_rows.shape, BF)
+    return pl.pallas_call(
+        expert_kernel,
+        out_shape=(rows, rows, jax.ShapeDtypeStruct(w_all.shape, BF)),
+        in_specs=[vmem] * 3,
+        out_specs=(vmem,) * 3,
+        compiler_params=pltpu.CompilerParams(vmem_limit_bytes=24 << 20),
+        name="expert_math",
+    )(token_rows, scaled_rows, w_all)
 
 
 def scatter_kernel(nz, ny, nx, chunks, out_ref, dx_ref, g_ref, expand_ref,
@@ -220,16 +260,13 @@
         return push(y_out.at[target, :, cols], back_ref.at[y, :, cols], y_send.at[j, k - 1],
                     y_recv.at[j, k - 1], {"y": target})
 
-    def z_part(way, s):
-        return pl.ds(way * half, half) if s == 0 else pl.ds(0, block)
-
     def z_dest(way, s):
         return lax.rem(z + (nz // 2 - s if way == 0 else nz // 2 + s), nz)
 
-    def z_copy(way, s):
-        part = z_part(way, s)
-        src = g_ref.at[z_dest(way, s), part, :] if s == 0 else z_out.at[way, s - 1]
-        return push(src, z_in.at[way, s, part, :], z_send.at[way, s], z_recv.at[way, s],
+    def z_copy(way, s, q):
+        part = pl.ds(q * half, half)
+        src = g_ref.at[z_dest(way, s), part, :] if s == 0 else z_out.at[way, s - 1, part, :]
+        return push(src, z_in.at[way, s, part, :], z_send.at[way, s, q], z_recv.at[way, s, q],
                     {"dp": z_right if way == 0 else z_left})
 
     started = []
@@ -238,17 +275,16 @@
         copy.start()
         started.append(copy)
 
-    def z_next(s):
+    def z_next(s, k):
         for way in range(2):
-            z_copy(way, s - 1).wait_recv()
-            dest = z_dest(way, s)
-            for k in range(2):
-                rows_k = pl.ds(k * half, half)
-                value = g_ref[dest, rows_k, :]
-                if s > 1 or k == way:
-                    value = (value.astype(F32) + z_in[way, s - 1, rows_k, :].astype(F32)).astype(BF)
-                z_out[way, s - 1, rows_k, :] = value
-            start(z_copy(way, s))
+            q = 1 - way if k == 0 else way
+            part = pl.ds(q * half, half)
+            value = g_ref[z_dest(way, s), part, :]
+            if s > 1 or q == way:
+                z_copy(way, s - 1, q).wait_recv()
+                value = (value.astype(F32) + z_in[way, s - 1, part, :].astype(F32)).astype(BF)
+            z_out[way, s - 1, part, :] = value
+            start(z_copy(way, s, q))
 
     def chip_sum(j, h, owner):
         cols = pl.ds(j * step, step)
@@ -292,23 +328,24 @@
         for h in range(2):
             start(pair_copy(j, h))
     for way in range(2):
-        start(z_copy(way, 0))
-    z_steps = list(range(1, last + 1))
+        start(z_copy(way, 0, way))
+    z_steps = [(s, k) for s in range(1, last + 1) for k in range(2)]
     for j in range(chunks):
         first(j)
         if j >= 1:
             middle(j - 1)
         if j >= 2:
             finish(j - 2)
-        if j >= 1 and z_steps:
-            z_next(z_steps.pop(0))
+        if z_steps:
+            z_next(*z_steps.pop(0))
     middle(chunks - 1)
     for j in range(max(chunks - 2, 0), chunks):
         finish(j)
-    for s in z_steps:
-        z_next(s)
+    for s, k in z_steps:
+        z_next(s, k)
     for way in range(2):
-        z_copy(way, last).wait_recv()
+        for q in range(2):
+            z_copy(way, last, q).wait_recv()
     hid = dg_ref.shape[1]
     for k, ref in enumerate((dg_ref, du_ref, dd_ref)):
         cols = pl.ds(k * hid, hid)
@@ -327,7 +364,7 @@
     nz, ny, nx = lax.axis_size("dp"), lax.axis_size("y"), lax.axis_size("x")
     rows, width = out_part.shape[2:]
     block, cols = grads.shape[1:]
-    chunks = 4
+    chunks = 7
     vmem = pl.BlockSpec(memory_space=pltpu.VMEM)
     sems = pltpu.SemaphoreType.DMA
     grad = jax.ShapeDtypeStruct((block, cols // 3), BF)
@@ -349,10 +386,10 @@
             sems((chunks, 2)), sems((chunks, 2)),
             sems((chunks, 2, 2)), sems((chunks, 2, 2)),
             sems((chunks, ny - 1)), sems((chunks, ny - 1)),
-            sems((2, nz // 2)), sems((2, nz // 2)),
+            sems((2, nz // 2, 2)), sems((2, nz // 2, 2)),
         ],
         compiler_params=pltpu.CompilerParams(
-            collective_id=1, has_side_effects=True, vmem_limit_bytes=48 << 20
+            collective_id=1, has_side_effects=True, vmem_limit_bytes=26 << 20
         ),
         name="scatter_sums",
     )(out_part, dx_part, grads, squeeze_matrix(ny).T)
@@ -396,28 +433,7 @@
     token_rows = token_rows.reshape(n_slices * rows, width)
     scaled_rows = scaled_rows.reshape(n_slices * rows, width)
     w_all = w_all.reshape(width, 3 * hid)
-    w_gate, w_up, w_down = w_all[:, :hid], w_all[:, hid : 2 * hid], w_all[:, 2 * hid :]
-
-    gate_pre = dot(token_rows, w_gate)
-    up_pre = dot(token_rows, w_up)
-    sig = jax.nn.sigmoid(gate_pre)
-    active = gate_pre * sig
-    hidden = (active * up_pre).astype(BF)
-    d_hidden = dot(scaled_rows, w_down)
-    d_gate_pre = (d_hidden * up_pre * sig * (1.0 + gate_pre * (1.0 - sig))).astype(BF)
-    d_up_pre = (d_hidden * active).astype(BF)
-    out_part = dot(hidden, w_down, CONTRACT_COLS).astype(BF)
-    dx_part = (
-        dot(d_gate_pre, w_gate, CONTRACT_COLS) + dot(d_up_pre, w_up, CONTRACT_COLS)
-    ).astype(BF)
-    grads = jnp.concatenate(
-        [
-            dot(token_rows, d_gate_pre, CONTRACT_ROWS),
-            dot(token_rows, d_up_pre, CONTRACT_ROWS),
-            dot(scaled_rows, hidden, CONTRACT_ROWS),
-        ],
-        axis=1,
-    ).astype(BF)
+    out_part, dx_part, grads = expert_math(token_rows, scaled_rows, w_all)
     back, d_gate_w, d_up_w, d_down_w = scatter(
         out_part.reshape(n_slices // 2, 2, rows, width),
         dx_part.reshape(n_slices // 2, 2, rows, width),

time: 138 us -> 107 us (0.78)
  matrix products: 18.6 us -> 4.33 us
  local copies, waits for them, and re-layouts: 13.8 us -> 2.72 us
  Pallas kernels: 100 us -> 96.7 us
  other arithmetic: 3.57 us -> 1.68 us
    dot_general x16 -> x7, matrix products: 18.6 us -> 4.33 us  [dot(): return lax.dot_general(a, b, dims, preferred_element_type=F32)]
    dot_general x2 -> x0, local copies, waits for them, and re-layouts: 9.28 us -> none  [dot(): return lax.dot_general(a, b, dims, preferred_element_type=F32)]
    pallas_call x1, Pallas kernels: 47.3 us -> 38.8 us  [scatter(): pl.pallas_call(functools.partial(scatter_kernel, nz, ny, nx, chunks), out...]
    pallas_call x0 -> x1, Pallas kernels: none -> 4.59 us  [expert_math(): pl.pallas_call(expert_kernel, out_shape=(rows, rows, jax.ShapeDtypeStruct...]
    concatenate x1 -> x0, other arithmetic: 1.93 us -> none  [shards(): jnp.concatenate([dot(token_rows, d_gate_pre, CONTRACT_ROWS), dot(token_ro...]
    unnamed x27 -> x19, local copies, waits for them, and re-layouts: 4.3 us -> 2.54 us
where the time goes in v4:
time: 107 us; the launch traced here: 106 us
  Pallas kernels  96.7 us (90%)
  matrix products  4.33 us (4%)
  local copies, waits for them, and re-layouts  2.72 us (3%)
  other arithmetic  1.68 us (2%)
    pallas_call x1, Pallas kernels, gather(): pl.pallas_call(functools.partial(gather_kernel, nz, ny, nx, chunks), out_...  53.3 us
    pallas_call x1, Pallas kernels, scatter(): pl.pallas_call(functools.partial(scatter_kernel, nz, ny, nx, chunks), out...  38.8 us
    pallas_call x1, Pallas kernels, expert_math(): pl.pallas_call(expert_kernel, out_shape=(rows, rows, jax.ShapeDtypeStruct...  4.59 us
    dot_general x7, matrix products, dot(): return lax.dot_general(a, b, dims, preferred_element_type=F32)  4.33 us
    unnamed x19, local copies, waits for them, and re-layouts  2.54 us

profile of v4, /device:TPU:1, one launch (start us, length us, event | category | flops | bytes accessed | tf_op | source)
XLA Modules:
  0.0 106.3 jit_solution(11245379888058112048)
XLA Ops:
  0.6 0.0 copy-start
  0.7 0.8 convert_reduce_fusion
  1.5 0.1 convolution_select_fusion
  1.6 0.1 fusion.10
  1.7 0.1 mul.27
  1.8 0.1 eq.45
  1.9 0.3 fusion.4
  2.3 0.0 copy-start.2
  2.3 0.3 fusion.5
  2.7 0.1 pad_maximum_fusion.send_ref
  2.7 0.4 copy-done.4
  3.2 0.1 copy-done.5
  3.2 0.1 copy-done.6
  3.4 53.3 %gather_rows.1 = (bf16[8,48,3584]{2,1,0:T(8,128)(2,1)S(1)}, bf16[8,48,3584]{2,1,0:T(8,128)(2,1)S(1)}, bf16[8,448,384]{2,1,0:T(8,128)(2,1)S(1)}) custom-call(bf16[8,16,3584]{2,1,0:T(8,128)(2,1)S(1)} %pad_maximum_fusion.send_ref, bf16[448,384]{1,0:T(8,128)(2,1)S(1)} %pad_maximum_fusion.1.w_ref, bf16[96,128]{1,0:T(8,128)(2,1)S(1)} %copy-done.2), custom_call_target="tpu_custom_call" | custom-call | tf_op jit(solution)/shard_map/gather_rows/pallas_call | solution.py:161
  56.7 4.6 %expert_math.1 = (bf16[384,3584]{1,0:T(8,128)(2,1)S(1)}, bf16[384,3584]{1,0:T(8,128)(2,1)S(1)}, bf16[3584,384]{1,0:T(8,128)(2,1)S(1)}) custom-call(bf16[384,3584]{1,0:T(8,128)(2,1)S(1)} %bitcast.47, bf16[384,3584]{1,0:T(8,128)(2,1)S(1)} %bitcast.48, bf16[3584,384]{1,0:T(8,128)(2,1)S(1)} %bitcast.49), custom_call_target="tpu_custom_call" | custom-call | tf_op jit(solution)/shard_map/expert_math/pallas_call | solution.py:208
  61.3 38.8 %scatter_sums.1 = (bf16[8,16,3584]{2,1,0:T(8,128)(2,1)S(1)}, bf16[448,128]{1,0:T(8,128)(2,1)S(1)}, bf16[448,128]{1,0:T(8,128)(2,1)S(1)}, bf16[448,128]{1,0:T(8,128)(2,1)S(1)}) custom-call(bf16[4,2,48,3584]{3,2,1,0:T(8,128)(2,1)S(1)} %bitcast.44, bf16[4,2,48,3584]{3,2,1,0:T(8,128)(2,1)S(1)} %bitcast.45, bf16[8,448,384]{2,1,0:T(8,128)(2,1)S(1)} %bitcast.46, ...), custom_call_target="tpu_custom_call" | custom-call | tf_op jit(solution)/shard_map/scatter_sums/pallas_call | solution.py:371
  100.1 0.4 convolution_bitcast_fusion.1
  100.6 1.4 %fusion.1 = bf16[128,3584]{1,0:T(8,128)(2,1)} fusion(f32[128,3584]{1,0:T(8,128)S(1)} %convolution_bitcast_fusion.1, bf16[8,16,3584]{2,1,0:T(8,128)(2,1)S(1)} %get-tuple-element.22, f32[8,8,128]{2,1,0:T(8,128)S(1)} %get-tuple-element.28), kind=kOutput, calls=%fused_computation.4 | convolution fusion | flops 118358016 | bytes 3702784 | tf_op jit(solution)/shard_map/dot_general | solution.py:21
  101.9 1.3 %fusion.2 = bf16[128,3584]{1,0:T(8,128)(2,1)} fusion(bf16[8,16,3584]{2,1,0:T(8,128)(2,1)S(1)} %get-tuple-element.22, bf16[8,8,128]{2,1,0:T(8,128)(2,1)S(1)} %get-tuple-element.31), kind=kOutput, calls=%fused_computation.5 | convolution fusion | flops 117899264 | bytes 1851392 | tf_op jit(solution)/shard_map/dot_general | solution.py:21
  103.3 0.4 bitcast_reduce_fusion
  103.7 0.6 select_reduce_fusion
  104.3 0.6 copy.23
  105.0 0.6 copy.24
  105.6 0.6 copy.25
  (15 shorter events, 0.1 us)
Async XLA Ops:
  0.6 1.3 %copy-start = (bf16[128,3584]{1,0:T(8,128)(2,1)S(1)}, bf16[128,3584]{1,0:T(8,128)(2,1)}, u32[]{:S(2)}) copy-start(bf16[128,3584]{1,0:T(8,128)(2,1)} %param.10) | copy-start | bytes 2752516
  0.6 1.6 %copy-start.3 = (bf16[128,3584]{1,0:T(8,128)(2,1)S(1)}, bf16[128,3584]{1,0:T(8,128)(2,1)}, u32[]{:S(2)}) copy-start(bf16[128,3584]{1,0:T(8,128)(2,1)} %param.9) | copy-start | bytes 2752516
  2.3 0.9 copy-start.4
  2.3 0.9 copy-start.5
  2.3 1.0 copy-start.6
  2.3 1.0 copy-start.2
  56.7 4.6 %copy-start.1 = (bf16[128,96]{1,0:T(8,128)(2,1)S(1)}, bf16[128,96]{1,0:T(8,128)(2,1)}, u32[]{:S(2)}) copy-start(bf16[128,96]{1,0:T(8,128)(2,1)} %constant.23.expand_ref) | copy-start | bytes 73732
  101.9 1.8 %copy-start.7 = (s32[128,8]{0,1:T(8,128)S(1)}, s32[128,8]{0,1:T(8,128)}, u32[]{:S(2)}) copy-start(s32[128,8]{0,1:T(8,128)} %param.11) | copy-start | bytes 12292

commit v5 on v4

--- a/solution.py
+++ b/solution.py
@@ -134,7 +134,7 @@
             pass_near(j - 1)
         if j >= 2:
             pass_far(j - 2)
-        if j >= 2 and z_steps:
+        if j >= 1 and z_steps:
             z_next(*z_steps.pop(0))
     pass_near(chunks - 1)
     for s, k in z_steps:
@@ -216,7 +216,7 @@
 
 
 def scatter_kernel(nz, ny, nx, chunks, out_ref, dx_ref, g_ref, expand_ref,
-                   back_ref, dg_ref, du_ref, dd_ref,
+                   back_ref, sum_ref,
                    pair, far_out, far_in, near_out, near_in, y_out, z_out, z_in,
                    pair_send, pair_recv, far_send, far_recv, near_send, near_recv,
                    y_send, y_recv, z_send, z_recv):
@@ -346,13 +346,10 @@
     for way in range(2):
         for q in range(2):
             z_copy(way, last, q).wait_recv()
-    hid = dg_ref.shape[1]
-    for k, ref in enumerate((dg_ref, du_ref, dd_ref)):
-        cols = pl.ds(k * hid, hid)
-        total = g_ref[z, :, cols].astype(F32)
-        for way in range(2):
-            total = total + z_in[way, last, :, cols].astype(F32)
-        ref[...] = total.astype(BF)
+    total = g_ref[z].astype(F32)
+    for way in range(2):
+        total = total + z_in[way, last].astype(F32)
+    sum_ref[...] = total.astype(BF)
     for j in range(chunks):
         for k in range(1, ny):
             y_copy(j, k).wait_recv()
@@ -367,12 +364,12 @@
     chunks = 7
     vmem = pl.BlockSpec(memory_space=pltpu.VMEM)
     sems = pltpu.SemaphoreType.DMA
-    grad = jax.ShapeDtypeStruct((block, cols // 3), BF)
+    grad = jax.ShapeDtypeStruct((block, cols), BF)
     return pl.pallas_call(
         functools.partial(scatter_kernel, nz, ny, nx, chunks),
-        out_shape=(jax.ShapeDtypeStruct((ny, 2 * PAD, width), BF), grad, grad, grad),
+        out_shape=(jax.ShapeDtypeStruct((ny, 2 * PAD, width), BF), grad),
         in_specs=[vmem] * 4,
-        out_specs=(vmem,) * 4,
+        out_specs=(vmem,) * 2,
         scratch_shapes=[
             pltpu.VMEM((2, nx, rows, width), BF),
             pltpu.VMEM((2, rows, width), BF),
@@ -434,7 +431,7 @@
     scaled_rows = scaled_rows.reshape(n_slices * rows, width)
     w_all = w_all.reshape(width, 3 * hid)
     out_part, dx_part, grads = expert_math(token_rows, scaled_rows, w_all)
-    back, d_gate_w, d_up_w, d_down_w = scatter(
+    back, summed = scatter(
         out_part.reshape(n_slices // 2, 2, rows, width),
         dx_part.reshape(n_slices // 2, 2, rows, width),
         grads.reshape(width // gate_w.shape[0], gate_w.shape[0], 3 * hid),
@@ -452,6 +449,7 @@
     inner = dot(back, cotangent, CONTRACT_COLS) * member_out
     by_expert = jnp.sum(inner.reshape(groups, 2 * PAD, tok_rows), axis=1).T
     d_gates = jnp.sum(jnp.where(match, by_expert[:, None, :], 0.0), axis=2)
+    d_gate_w, d_up_w, d_down_w = jnp.split(summed, 3, axis=1)
     return moe_out, d_tokens, d_gates, d_gate_w, d_up_w, d_down_w
 
 

time: 107 us -> 106 us (level)
  local copies, waits for them, and re-layouts: 2.72 us -> 1.53 us
    unnamed x19 -> x16, local copies, waits for them, and re-layouts: 2.54 us -> 0.61 us
where the time goes in v5:
time: 106 us; the launch traced here: 105 us
  Pallas kernels  96.5 us (91%)
  matrix products  4.32 us (4%)
  other arithmetic  1.68 us (2%)
  local copies, waits for them, and re-layouts  1.53 us (1%)
    pallas_call x1, Pallas kernels, gather(): pl.pallas_call(functools.partial(gather_kernel, nz, ny, nx, chunks), out_...  53.3 us
    pallas_call x1, Pallas kernels, scatter(): pl.pallas_call(functools.partial(scatter_kernel, nz, ny, nx, chunks), out...  38.5 us
    pallas_call x1, Pallas kernels, expert_math(): pl.pallas_call(expert_kernel, out_shape=(rows, rows, jax.ShapeDtypeStruct...  4.59 us
    dot_general x7, matrix products, dot(): return lax.dot_general(a, b, dims, preferred_element_type=F32)  4.32 us

profile of v5, /device:TPU:1, one launch (start us, length us, event | category | flops | bytes accessed | tf_op | source)
XLA Modules:
  0.0 104.8 jit_solution(9360633180625049908)
XLA Ops:
  0.6 0.0 copy-start
  0.7 0.8 convert_reduce_fusion
  1.5 0.1 convolution_select_fusion
  1.6 0.1 fusion.10
  1.7 0.1 mul.27
  1.8 0.1 eq.45
  1.9 0.3 fusion.4
  2.3 0.0 copy-start.5
  2.3 0.0 copy-start.2
  2.3 0.3 fusion.5
  2.7 0.1 pad_maximum_fusion.send_ref
  2.7 0.4 copy-done.4
  3.2 0.1 copy-done.5
  3.2 0.1 copy-done.6
  3.4 53.3 %gather_rows.1 = (bf16[8,48,3584]{2,1,0:T(8,128)(2,1)S(1)}, bf16[8,48,3584]{2,1,0:T(8,128)(2,1)S(1)}, bf16[8,448,384]{2,1,0:T(8,128)(2,1)S(1)}) custom-call(bf16[8,16,3584]{2,1,0:T(8,128)(2,1)S(1)} %pad_maximum_fusion.send_ref, bf16[448,384]{1,0:T(8,128)(2,1)S(1)} %pad_maximum_fusion.1.w_ref, bf16[96,128]{1,0:T(8,128)(2,1)S(1)} %copy-done.2), custom_call_target="tpu_custom_call" | custom-call | tf_op jit(solution)/shard_map/gather_rows/pallas_call | solution.py:161
  56.7 0.0 copy-start.1
  56.7 4.6 %expert_math.1 = (bf16[384,3584]{1,0:T(8,128)(2,1)S(1)}, bf16[384,3584]{1,0:T(8,128)(2,1)S(1)}, bf16[3584,384]{1,0:T(8,128)(2,1)S(1)}) custom-call(bf16[384,3584]{1,0:T(8,128)(2,1)S(1)} %bitcast.44, bf16[384,3584]{1,0:T(8,128)(2,1)S(1)} %bitcast.45, bf16[3584,384]{1,0:T(8,128)(2,1)S(1)} %bitcast.46), custom_call_target="tpu_custom_call" | custom-call | tf_op jit(solution)/shard_map/expert_math/pallas_call | solution.py:208
  61.3 38.5 %scatter_sums.1 = (bf16[8,16,3584]{2,1,0:T(8,128)(2,1)S(1)}, bf16[448,384]{1,0:T(8,128)(2,1)S(1)}) custom-call(bf16[4,2,48,3584]{3,2,1,0:T(8,128)(2,1)S(1)} %bitcast.47, bf16[4,2,48,3584]{3,2,1,0:T(8,128)(2,1)S(1)} %bitcast.48, bf16[8,448,384]{2,1,0:T(8,128)(2,1)S(1)} %bitcast.49, bf16[128,96]{1,0:T(8,128)(2,1)S(1)} %copy-done.1), custom_call_target="tpu_custom_call" | custom-call | tf_op jit(solution)/shard_map/scatter_sums/pallas_call | solution.py:368
  99.9 0.4 convolution_bitcast_fusion.1
  100.3 1.3 %fusion.1 = bf16[128,3584]{1,0:T(8,128)(2,1)} fusion(f32[128,3584]{1,0:T(8,128)S(1)} %convolution_bitcast_fusion.1, bf16[8,16,3584]{2,1,0:T(8,128)(2,1)S(1)} %get-tuple-element.20, f32[8,8,128]{2,1,0:T(8,128)S(1)} %get-tuple-element.27), kind=kOutput, calls=%fused_computation.4 | convolution fusion | flops 118358016 | bytes 3702784 | tf_op jit(solution)/shard_map/dot_general | solution.py:21
  101.7 1.3 %fusion.2 = bf16[128,3584]{1,0:T(8,128)(2,1)} fusion(bf16[8,16,3584]{2,1,0:T(8,128)(2,1)S(1)} %get-tuple-element.20, bf16[8,8,128]{2,1,0:T(8,128)(2,1)S(1)} %get-tuple-element.30), kind=kOutput, calls=%fused_computation.5 | convolution fusion | flops 117899264 | bytes 1851392 | tf_op jit(solution)/shard_map/dot_general | solution.py:21
  103.0 0.7 fusion.21
  103.8 0.4 bitcast_reduce_fusion
  104.2 0.6 select_reduce_fusion
  (13 shorter events, 0.1 us)
Async XLA Ops:
  0.6 1.3 %copy-start = (bf16[128,3584]{1,0:T(8,128)(2,1)S(1)}, bf16[128,3584]{1,0:T(8,128)(2,1)}, u32[]{:S(2)}) copy-start(bf16[128,3584]{1,0:T(8,128)(2,1)} %param.10) | copy-start | bytes 2752516
  0.6 1.6 %copy-start.3 = (bf16[128,3584]{1,0:T(8,128)(2,1)S(1)}, bf16[128,3584]{1,0:T(8,128)(2,1)}, u32[]{:S(2)}) copy-start(bf16[128,3584]{1,0:T(8,128)(2,1)} %param.9) | copy-start | bytes 2752516
  2.3 0.9 copy-start.4
  2.3 0.9 copy-start.5
  2.3 1.0 copy-start.6
  2.3 1.0 copy-start.2
  56.7 4.6 %copy-start.1 = (bf16[128,96]{1,0:T(8,128)(2,1)S(1)}, bf16[128,96]{1,0:T(8,128)(2,1)}, u32[]{:S(2)}) copy-start(bf16[128,96]{1,0:T(8,128)(2,1)} %constant.23.expand_ref) | copy-start | bytes 73732
  101.7 2.5 %copy-start.7 = (s32[128,8]{0,1:T(8,128)S(1)}, s32[128,8]{0,1:T(8,128)}, u32[]{:S(2)}) copy-start(s32[128,8]{0,1:T(8,128)} %param.11) | copy-start | bytes 12292
